TPU v7x, 256 devices: a whole 4x4x8 slice. The times are simulated.
256 devices in a mesh: shell: 2 (over core), row: 8 (over z), col: 16 (over x, y).
Axes of the slice: x: 4, y: 4, z: 8, core: 2. Of those that a mesh axis runs over, the one named last changes fastest.
Arguments:
- convergence: bfloat16 [2, 16384, 16384], P('shell', ('row', 'col')), may hold values from -6 to 6
- lens_weight: float32 [2], P('shell'), may hold values from 0.3 to 1
- rays_in: float32 [6, 1024, 16384], P(None, ('row', 'col')), may hold values from -6 to 6
Outputs:
- rays_out: float32 [2, 6, 1024, 16384], P('shell', None, ('row', 'col'))
All inputs are finite; a program needn't handle non-finite values.
Results may differ from a plain program's by a relative error of at most 0.0003.
Values sent between devices are 32-bit elements; how exact they have to be, the bound alone decides.
A program may use at most 192 MiB of HBM per device.

v0:
```python
import math

import jax
import jax.numpy as jnp
from jax import lax
from jax.sharding import PartitionSpec as P

STRIDE = 16


HIGHEST = lax.Precision.HIGHEST
SPLIT_THREE = lax.Precision.HIGH


def passed_along(value, axis, steps):
    count = lax.axis_size(axis)
    leading, last = (max(0, -steps), min(count, count - steps))
    return lax.ppermute(value, axis, [(source, source + steps) for source in range(leading, last)])


def product(form, left, right):
    return jnp.einsum(form, left, right, precision=HIGHEST, preferred_element_type=jnp.float32)


def product_input(form, left, right):
    return jnp.einsum(form, left, right, precision=SPLIT_THREE, preferred_element_type=jnp.float32)


def counting(length):
    return jnp.arange(length, dtype=jnp.int32)


def phases(first, second, length, sign):
    whole = first[:, None] * second[None, :] % length
    angle = sign * 2.0 * math.pi / length * whole.astype(jnp.float32)
    return (jnp.cos(angle), jnp.sin(angle))


def complex_section(form, real, imaginary, table):
    cosine, sine = table
    return (
        product(form, real, cosine) - product(form, imaginary, sine),
        product(form, real, sine) + product(form, imaginary, cosine),
    )


def twiddle(real, imaginary, table):
    cosine, sine = table
    return (real * cosine - imaginary * sine, real * sine + imaginary * cosine)


def column_spectrum(field, devices):
    rows_dev, length = field.shape
    block = length // (2 * devices)
    shaped = field.reshape(rows_dev, block, 2 * devices)
    cosine, sine = phases(counting(block), counting(block), block, -1.0)
    real = product_input("rvu,vt->rtu", shaped, cosine)
    imaginary = product_input("rvu,vt->rtu", shaped, sine)
    real, imaginary = twiddle(
        real, imaginary, phases(counting(block), counting(2 * devices), length, -1.0)
    )
    real, imaginary = complex_section(
        "rtu,ub->btr",
        real,
        imaginary,
        phases(counting(2 * devices), counting(devices), 2 * devices, -1.0),
    )
    return jnp.stack([real, imaginary]).reshape(2, devices * block, rows_dev)


def row_spectrum(arrived, order, rows_dev):
    block, length = (arrived.shape[1], arrived.shape[2])
    devices = length // rows_dev
    real = arrived[0].reshape(block, devices, rows_dev)
    imaginary = arrived[1].reshape(block, devices, rows_dev)
    real, imaginary = complex_section(
        "tpn,pk->tkn", real, imaginary, phases(order, counting(devices), devices, -1.0)
    )
    real, imaginary = twiddle(
        real, imaginary, phases(counting(devices), counting(rows_dev), length, -1.0)
    )
    real, imaginary = complex_section(
        "tkn,nj->tjk",
        real,
        imaginary,
        phases(counting(rows_dev), counting(rows_dev), rows_dev, -1.0),
    )
    return (real.reshape(block, length), imaginary.reshape(block, length))


def potential(real, imaginary, first_bin):
    block, length = real.shape
    half = length // 2
    frequency = counting(length)
    signed = jnp.where(frequency < half, frequency, frequency - length).astype(jnp.float32)
    wave_rows = (2.0 * math.pi / length * signed)[None, :]
    wave_cols = (2.0 * math.pi / length * (first_bin + counting(block)).astype(jnp.float32))[
        :, None
    ]
    squared = wave_rows * wave_rows + wave_cols * wave_cols
    valid = (squared > 0.0) & (frequency != half)[None, :]
    scale = jnp.where(valid, -2.0 / jnp.where(valid, squared, 1.0), 0.0) / (
        float(length) * float(length)
    )
    return (real * scale, imaginary * scale, wave_rows, wave_cols)


def ray_rows(real, imaginary, rays_dev):
    fields, block, length = real.shape
    rays = length // STRIDE
    devices = rays // rays_dev
    real = (
        real.reshape(fields, block, STRIDE, rays)
        .sum(axis=2)
        .reshape(fields, block, rays_dev, devices)
    )
    imaginary = (
        imaginary.reshape(fields, block, STRIDE, rays)
        .sum(axis=2)
        .reshape(fields, block, rays_dev, devices)
    )
    real, imaginary = complex_section(
        "ftqp,qa->ftap",
        real,
        imaginary,
        phases(counting(rays_dev), counting(rays_dev), rays_dev, 1.0),
    )
    real, imaginary = twiddle(
        real, imaginary, phases(counting(rays_dev), counting(devices), rays, 1.0)
    )
    real, imaginary = complex_section(
        "ftap,pz->fzat", real, imaginary, phases(counting(devices), counting(devices), devices, 1.0)
    )
    joined = jnp.stack(
        [real.reshape(fields, rays, block), imaginary.reshape(fields, rays, block)], axis=2
    )
    return joined.reshape(fields, rays, 2 * block)


def column_fields(real, imaginary, order, length):
    devices, block = (real.shape[2], real.shape[3])
    bins = order[:, None] * block + counting(block)[None, :]
    weight = jnp.where(bins == 0, 1.0, 2.0).astype(jnp.float32)
    real, imaginary = complex_section(
        "fypt,pu->fytu",
        real * weight,
        imaginary * weight,
        phases(order, counting(2 * devices), 2 * devices, 1.0),
    )
    real, imaginary = twiddle(
        real, imaginary, phases(counting(block), counting(2 * devices), length, 1.0)
    )
    cosine, sine = phases(counting(block), counting(block), block, 1.0)
    result = product("fytu,tv->fyvu", real, cosine) - product("fytu,tv->fyvu", imaginary, sine)
    return result.reshape(result.shape[0], result.shape[1], length)


def advance(state, fields, weight):
    shift_rows = state[0] - weight * fields[0]
    shift_cols = state[1] - weight * fields[1]
    curve_rows, curve_cols, curve_mixed = (fields[2], fields[3], fields[4])
    upper_left, upper_right, lower_left, lower_right = (state[2], state[3], state[4], state[5])
    new_ul = upper_left - weight * (curve_rows * upper_left + curve_mixed * lower_left)
    new_ur = upper_right - weight * (curve_rows * upper_right + curve_mixed * lower_right)
    new_ll = lower_left - weight * (curve_mixed * upper_left + curve_cols * lower_left)
    new_lr = lower_right - weight * (curve_mixed * upper_right + curve_cols * lower_right)
    return jnp.stack([shift_rows, shift_cols, new_ul, new_ur, new_ll, new_lr])


def body(convergence, lens_weight, rays_in):
    rows_axis = lax.axis_size("row")
    cols_axis = lax.axis_size("col")
    devices = rows_axis * cols_axis
    shells_dev, rows_dev, length = convergence.shape
    block = length // (2 * devices)
    first_bin = (lax.axis_index("row") * cols_axis + lax.axis_index("col")) * block
    position = counting(devices)
    all_fields = []
    spectrum = column_spectrum(convergence[0], devices)
    arrived = lax.all_to_all(spectrum, ("row", "col"), split_axis=1, concat_axis=2, tiled=True)
    real, imaginary = row_spectrum(arrived, position, rows_dev)
    real, imaginary, wave_rows, wave_cols = potential(real, imaginary, first_bin)
    stacked_real = jnp.stack(
        [
            -wave_rows * imaginary,
            -wave_cols * imaginary,
            -wave_rows * wave_rows * real,
            -wave_cols * wave_cols * real,
            -wave_rows * wave_cols * real,
        ]
    )
    stacked_imaginary = jnp.stack(
        [
            wave_rows * real,
            wave_cols * real,
            -wave_rows * wave_rows * imaginary,
            -wave_cols * wave_cols * imaginary,
            -wave_rows * wave_cols * imaginary,
        ]
    )
    outgoing = ray_rows(stacked_real, stacked_imaginary, rows_dev // STRIDE)
    returned = lax.all_to_all(outgoing, ("row", "col"), split_axis=1, concat_axis=2, tiled=True)
    returned = returned.reshape(returned.shape[0], returned.shape[1], devices, 2, block)
    back_real = returned[:, :, :, 0, :]
    back_imaginary = returned[:, :, :, 1, :]
    all_fields.append(column_fields(back_real, back_imaginary, position, length))

    def run_local(start):
        current = start
        current = advance(current, all_fields[0], lens_weight[0])
        results = [current]
        return jnp.stack(results)

    shell_index = lax.axis_index("shell")
    outputs = run_local(rays_in)
    received = passed_along(outputs[-1], "shell", 1)
    outputs = jnp.where(shell_index == 1, run_local(received), outputs)
    return outputs


def solution(mesh):
    in_specs = (P("shell", ("row", "col"), None), P("shell"), P(None, ("row", "col"), None))
    out_specs = P("shell", None, ("row", "col"), None)
    return jax.shard_map(body, mesh=mesh, in_specs=in_specs, out_specs=out_specs, check_vma=False)
```

profile of v0, /device:TPU:1, one launch (start us, length us, event | category | flops | bytes accessed | tf_op | source)
XLA Modules:
  0.0 616.8 jit_solution(11229222205800042720)
XLA Ops:
  3.7 5.7 fusion.150
  9.4 6.9 %subtract_bitcast_fusion = (f32[128,64,256]{2,1,0:T(8,128)S(1)}, f32[128,64,256]{2,1,0:T(8,128)S(1)}) fusion(f32[64,128,256]{2,0,1:T(8,128)} %fusion.150, f32[64,256]{1,0:T(8,128)S(1)} %get-tuple-element.24, f32[64,256]{1,0:T(8,128)S(1)} %get-tuple-element.25, bf16[128,64,256]{2,1,0:T(8,128)(2,1)S(1)} %bitcast.255), kind=kOutput, calls=%fused_computation.3 | convolution fusion | flops 817946624 | bytes 29491200 | tf_op jit(solution)/shard_map/rvu,vt->rtu/dot_general | solution.py:26
  16.3 13.1 %fusion.2 = f32[128,128,64]{1,0,2:T(8,128)S(1)} fusion(f32[128,64,256]{2,1,0:T(8,128)S(1)} %get-tuple-element.14), kind=kOutput, calls=%fused_computation.6 | convolution fusion | flops 3221684224 | bytes 12582912 | tf_op jit(solution)/shard_map/rtu,ub->btr/dot_general | solution.py:22
  29.4 13.4 %fusion = f32[128,128,64]{1,0,2:T(8,128)S(1)} fusion(f32[128,64,256]{2,1,0:T(8,128)S(1)} %get-tuple-element.14), kind=kOutput, calls=%fused_computation.4 | convolution fusion | flops 3221684224 | bytes 12582912 | tf_op jit(solution)/shard_map/rtu,ub->btr/dot_general | solution.py:22
  42.8 13.3 %subtract_bitcast_fusion.2 = f32[128,64,128]{2,0,1:T(8,128)S(1)} fusion(f32[128,128,64]{1,0,2:T(8,128)S(1)} %fusion.2, f32[128,64,256]{2,1,0:T(8,128)S(1)} %get-tuple-element.13), kind=kOutput, calls=%fused_computation.45 | convolution fusion | flops 3222732800 | bytes 16777216 | tf_op jit(solution)/shard_map/rtu,ub->btr/dot_general | solution.py:22
  58.8 13.1 %add_bitcast_fusion.2 = f32[128,64,128]{2,0,1:T(8,128)S(1)} fusion(f32[128,128,64]{1,0,2:T(8,128)S(1)} %fusion, f32[128,64,256]{2,1,0:T(8,128)S(1)} %get-tuple-element.13), kind=kOutput, calls=%fused_computation.44 | convolution fusion | flops 3222732800 | bytes 16777216 | tf_op jit(solution)/shard_map/rtu,ub->btr/dot_general | solution.py:22
  75.4 31.3 %copy.75 = f32[2,8192,128]{2,0,1:T(2,128)} copy(f32[2,8192,128]{2,1,0:T(8,128)S(1)} %pad_maximum_fusion) | data formatting | bytes 16777216 | tf_op jit(solution)/shard_map/stack | solution.py:68
  106.6 17.0 %all-to-all-start = ((f32[2,8192,128]{2,0,1:T(2,128)}), f32[2,8192,128]{2,0,1:T(2,128)}, u32[]{:S(2)}, u32[]{:S(2)}) async-start(f32[2,8192,128]{2,0,1:T(2,128)} %copy.75), calls=%async_computation | async-start | bytes 16777216 | tf_op jit(solution)/shard_map/all_to_all | solution.py:180
  124.2 182.3 %all-to-all-done = f32[2,8192,128]{2,0,1:T(2,128)} async-done(((f32[2,8192,128]{2,0,1:T(2,128)}), f32[2,8192,128]{2,0,1:T(2,128)}, u32[]{:S(2)}, u32[]{:S(2)}) %all-to-all-start) | async-done | bytes 8388640 | tf_op jit(solution)/shard_map/all_to_all | solution.py:180
  306.5 8.2 %copy.149 = f32[2,128,64,128]{3,1,2,0:T(8,128)S(1)} copy(f32[2,128,64,128]{3,0,2,1:T(2,128)} %bitcast.19) | data formatting | bytes 16777216 | tf_op jit(solution)/shard_map/all_to_all | solution.py:180
  314.7 4.4 fusion.23
  319.1 4.8 fusion.22
  323.9 4.4 fusion.34
  328.3 4.4 fusion.35
  332.8 5.0 fusion.15
  337.8 6.1 fusion.13
  343.9 6.2 %add_bitcast_fusion.1 = f32[64,128,128]{2,1,0:T(8,128)} fusion(f32[128,64,128]{2,0,1:T(8,128)S(1)} %fusion.15, f32[128,64,128]{2,0,1:T(8,128)S(1)} %fusion.35, f32[128,64,128]{2,0,1:T(8,128)S(1)} %fusion.34, f32[128,128]{1,0:T(8,128)S(1)} %get-tuple-element.26, f32[128,128]{1,0:T(8,128)S(1)} %get-tuple-element.27), kind=kOutput, calls=%fused_computation.41 | convolution fusion | flops 1615036416 | bytes 16908288 | tf_op jit(solution)/shard_map/tkn,nj->tjk/dot_general | solution.py:22
  350.2 4.9 reshape.1031
  355.0 11.1 %subtract_bitcast_fusion.1 = f32[64,128,128]{2,1,0:T(8,128)} fusion(f32[128,64,128]{2,0,1:T(8,128)} %fusion.13, f32[128,64,128]{2,0,1:T(8,128)} %copy-done.3, f32[128,64,128]{2,0,1:T(8,128)} %copy-done.2, f32[128,128]{1,0:T(8,128)S(1)} %get-tuple-element.26, f32[128,128]{1,0:T(8,128)S(1)} %get-tuple-element.27), kind=kOutput, calls=%fused_computation.38 | convolution fusion | flops 1615036416 | bytes 16908288 | tf_op jit(solution)/shard_map/tkn,nj->tjk/dot_general | solution.py:22
  366.1 5.1 reshape.1032
  371.3 4.0 multiply_dynamic-update-slice_fusion.3
  381.1 4.1 fusion.12
  385.2 4.3 multiply_dynamic-update-slice_fusion.6
  389.5 4.7 multiply_dynamic-update-slice_fusion.5
  394.1 3.8 multiply_dynamic-update-slice_fusion.4
  401.3 9.5 %reduce_sum.18 = f32[5,64,1024]{2,1,0:T(8,128)S(1)} reduce(f32[5,64,16,1024]{3,2,1,0:T(8,128)} %fusion.11, f32[]{:T(128)} %constant.177.clone.1), dimensions={2}, to_apply=%region_0.1 | reduce | flops 4915200 | bytes 22282244 | tf_op jit(solution)/shard_map/reduce_sum | solution.py:114
  413.4 9.7 %reduce_sum.19 = f32[5,64,1024]{2,1,0:T(8,128)S(1)} reduce(f32[5,64,16,1024]{3,2,1,0:T(8,128)} %copy-done.4, f32[]{:T(128)} %constant.177.clone.1), dimensions={2}, to_apply=%region_1.2 | reduce | flops 4915200 | bytes 22282244 | tf_op jit(solution)/shard_map/reduce_sum | solution.py:119
  441.8 4.5 pad_maximum_fusion.1
  446.2 4.2 copy.92
  454.0 12.4 %all-to-all-start.1 = ((f32[5,1024,128]{2,0,1:T(8,128)}), f32[5,1024,128]{2,0,1:T(8,128)}, u32[]{:S(2)}, u32[]{:S(2)}) async-start(f32[5,1024,128]{2,0,1:T(8,128)} %copy.93), calls=%async_computation.1 | async-start | bytes 8388608 | tf_op jit(solution)/shard_map/all_to_all | solution.py:202
  467.3 91.9 %all-to-all-done.1 = f32[5,1024,128]{2,0,1:T(8,128)} async-done(((f32[5,1024,128]{2,0,1:T(8,128)}), f32[5,1024,128]{2,0,1:T(8,128)}, u32[]{:S(2)}, u32[]{:S(2)}) %all-to-all-start.1) | async-done | bytes 2621472 | tf_op jit(solution)/shard_map/all_to_all | solution.py:202
  597.6 9.2 %collective-permute-done = f32[6,8,16384]{2,1,0:T(8,128)} collective-permute-done((f32[6,8,16384]{2,1,0:T(8,128)}, f32[6,8,16384]{2,1,0:T(8,128)}, u32[]{:S(2)}, u32[]{:S(2)}) %collective-permute-start) | collective-permute-done | bytes 3145760 | tf_op jit(solution)/shard_map/ppermute | solution.py:18
  (84 shorter events, 92.0 us)
Async XLA Ops:
  106.6 199.8 %all-to-all-start = ((f32[2,8192,128]{2,0,1:T(2,128)}), f32[2,8192,128]{2,0,1:T(2,128)}, u32[]{:S(2)}, u32[]{:S(2)}) async-start(f32[2,8192,128]{2,0,1:T(2,128)} %copy.75), calls=%async_computation | async-start | bytes 16777216 | tf_op jit(solution)/shard_map/all_to_all | solution.py:180
  328.3 15.6 %copy-start.2 = (f32[128,64,128]{2,0,1:T(8,128)}, f32[128,64,128]{2,0,1:T(8,128)S(1)}, u32[]{:S(2)}) copy-start(f32[128,64,128]{2,0,1:T(8,128)S(1)} %fusion.34) | copy-start | bytes 12582916
  332.8 11.2 %copy-start.3 = (f32[128,64,128]{2,0,1:T(8,128)}, f32[128,64,128]{2,0,1:T(8,128)S(1)}, u32[]{:S(2)}) copy-start(f32[128,64,128]{2,0,1:T(8,128)S(1)} %fusion.35) | copy-start | bytes 12582916
  371.3 4.1 copy-start
  375.4 2.2 copy-start.1
  385.2 12.8 %copy-start.4 = (f32[5,64,16,1024]{3,2,1,0:T(8,128)}, f32[5,64,16,1024]{3,2,1,0:T(8,128)S(1)}, u32[]{:S(2)}) copy-start(f32[5,64,16,1024]{3,2,1,0:T(8,128)S(1)} %get-tuple-element.15) | copy-start | bytes 62914564
  423.1 1.5 copy-start.7
  438.5 3.3 copy-start.6
  454.0 105.2 %all-to-all-start.1 = ((f32[5,1024,128]{2,0,1:T(8,128)}), f32[5,1024,128]{2,0,1:T(8,128)}, u32[]{:S(2)}, u32[]{:S(2)}) async-start(f32[5,1024,128]{2,0,1:T(8,128)} %copy.93), calls=%async_computation.1 | async-start | bytes 8388608 | tf_op jit(solution)/shard_map/all_to_all | solution.py:202
  584.2 6.1 copy-start.5
  596.3 10.5 %collective-permute-start = (f32[6,8,16384]{2,1,0:T(8,128)}, f32[6,8,16384]{2,1,0:T(8,128)}, u32[]{:S(2)}, u32[]{:S(2)}) collective-permute-start(f32[6,8,16384]{2,1,0:T(8,128)} %constant_dynamic-update-slice_fusion), channel_id=1, source_target_pairs={{0,128},{1,129},{2,130},{3,131},{4,132},{5,133},{6,134},{7,135},{8... | collective-permute-start | bytes 9437192 | tf_op jit(solution)/shard_map/ppermute | solution.py:18
  610.3 4.1 copy-start.8
where the time goes:
time: 622 us; the launch traced here: 617 us
  waiting for transfers between devices  283 us (45%)
  matrix products  143 us (23%)
  local copies, waits for them, and re-layouts  81 us (13%)
  other arithmetic  77.1 us (12%)
  starting transfers between devices  30.7 us (5%)
    all_to_all x1, waiting for transfers between devices, body(): lax.all_to_all(spectrum, ('row', 'col'), split_axis=1, concat_axis=2, til...  182 us
    dot_general x26, matrix products, product(): jnp.einsum(form, left, right, precision=HIGHEST, preferred_element_type=j...  130 us
    all_to_all x1, waiting for transfers between devices, body(): lax.all_to_all(outgoing, ('row', 'col'), split_axis=1, concat_axis=2, til...  91.9 us
    unnamed x19, other arithmetic  40 us
    another operation x1, local copies, waits for them, and re-layouts, column_spectrum(): return jnp.stack([real, imaginary]).reshape(2, devices * block, rows_dev)  31.3 us
    all_to_all x1, starting transfers between devices, body(): lax.all_to_all(spectrum, ('row', 'col'), split_axis=1, concat_axis=2, til...  17 us
    dot_general x2, matrix products, product_input(): jnp.einsum(form, left, right, precision=SPLIT_THREE, preferred_element_ty...  12.6 us
  transfers between devices with their start and end apart: 3, of which 3 were waited for; matrix products, arithmetic and copies ran while one was open for 0% of the time, Pallas kernels for 0%

commit v1 on v0

v1 whole, which is shorter than its diff:
```python
import math

import jax
import jax.numpy as jnp
import ml_dtypes
import numpy as np
from jax import lax
from jax.experimental import pallas as pl
from jax.experimental.pallas import tpu as pltpu
from jax.sharding import PartitionSpec as P


N = 16384
CHUNKS = 4
PER_CHUNK = 4 // CHUNKS
HELD = 16 * PER_CHUNK
ROWS = 32 * PER_CHUNK + 8
STEP = 2.0 * math.pi / N


def halves(table):
    table = np.asarray(table, np.float32)
    high = table.astype(ml_dtypes.bfloat16)
    low = (table - high.astype(np.float32)).astype(ml_dtypes.bfloat16)
    return high, low


def right_table(table):
    high, low = halves(table)
    return np.concatenate([high, high, low], axis=-2)


def left_table(table):
    high, low = halves(table)
    return np.concatenate([high, high, low], axis=-1)


def turns(first, second, length, sign):
    whole = np.outer(first, second) % length
    angle = sign * 2.0 * np.pi * whole / length
    return np.cos(angle), np.sin(angle)


def complex_right(first, second, length, sign):
    cosine, sine = turns(first, second, length, sign)
    return np.block([[cosine, sine], [-sine, cosine]])


def bins_of(chunk):
    return np.array([4 * y + PER_CHUNK * chunk + k for y in range(16) for k in range(PER_CHUNK)])


def forward_tables(chunk):
    t = bins_of(chunk)
    cosine, sine = turns(t, np.arange(64), 64, -1)
    high, low = halves(np.concatenate([cosine, sine], axis=0))
    first = np.concatenate([high, low], axis=1)
    twist = np.stack(turns(t, np.arange(256), N, -1)).astype(np.float32)
    second = right_table(complex_right(np.arange(256), np.arange(128), 256, -1))
    return first, twist, second


def row_tables():
    k = np.arange(128)
    grid = np.stack([right_table(complex_right(k, k + 128 * j, 1024, -1)) for j in range(8)])
    twist = np.zeros((8, 32, 128), np.float32)
    waves = np.zeros((8, 40, 128), np.float32)
    for j in range(8):
        base = k + 128 * j
        cosine, sine = turns(np.arange(16), base, N, -1)
        twist[j, 0::2], twist[j, 1::2] = cosine, sine
        for a in range(16):
            signed = base + 1024 * a - (N if a >= 8 else 0)
            wave = (2.0 * np.pi / N * signed).astype(np.float32)
            waves[j, a] = wave
            waves[j, 16 + a] = wave * wave
        waves[j, 32] = (base != 0).astype(np.float32)
    back = np.zeros((8, 16, 128), np.float32)
    for z in range(8):
        cosine, sine = turns(np.arange(8) - 128 * z, k, 1024, 1)
        back[z, 0::2], back[z, 1::2] = cosine * (-2.0 / N / N), sine * (-2.0 / N / N)
    cosine, sine = turns(k, k, 128, 1)
    left = left_table(np.block([[cosine, -sine], [sine, cosine]]))
    return grid, twist, waves, back, left


def final_tables():
    t = np.array([4 * y + k for k in range(4) for y in range(16)])
    first = right_table(complex_right(np.arange(128), np.arange(256), 256, 1))
    twist = np.stack(turns(t, np.arange(256), N, 1)).astype(np.float32)
    cosine, sine = turns(np.arange(64), t, 64, 1)
    second = left_table(np.concatenate([cosine, -sine], axis=1))
    bins = 64 * np.arange(128)[None, :] + t[:, None]
    wave = (2.0 * np.pi / N * bins).astype(np.float32)
    weight = np.where(bins == 0, 1.0, 2.0).astype(np.float32)
    scales = np.stack([weight, weight * wave, weight * wave * wave]).astype(np.float32)
    return first, twist, second, scales


def dot(left, right):
    return jnp.dot(left, right, preferred_element_type=jnp.float32)


def split(value):
    high = value.astype(jnp.bfloat16)
    low = (value - high.astype(jnp.float32)).astype(jnp.bfloat16)
    return high, low


def times(x, cosine, sine):
    return x[0] * cosine - x[1] * sine, x[0] * sine + x[1] * cosine


def plus(x, y):
    return x[0] + y[0], x[1] + y[1]


def minus(x, y):
    return x[0] - y[0], x[1] - y[1]


def quarter(x, sign):
    return (-x[1], x[0]) if sign > 0 else (x[1], -x[0])


def turned(x, eighths, sign):
    eighths %= 16
    if eighths == 0:
        return x
    if eighths == 4:
        return quarter(x, sign)
    if eighths == 2 or eighths == 6:
        root = math.sqrt(0.5)
        real, imaginary = x if eighths == 2 else quarter(x, sign)
        if sign > 0:
            return (real - imaginary) * root, (real + imaginary) * root
        return (real + imaginary) * root, (imaginary - real) * root
    angle = sign * 2.0 * math.pi * eighths / 16
    return times(x, math.cos(angle), math.sin(angle))


def four(x, sign):
    a, b = plus(x[0], x[2]), minus(x[0], x[2])
    c, d = plus(x[1], x[3]), quarter(minus(x[1], x[3]), sign)
    return [plus(a, c), plus(b, d), minus(a, c), minus(b, d)]


def sixteen(x, sign):
    inner = [four([x[4 * p + q] for p in range(4)], sign) for q in range(4)]
    out = [None] * 16
    for a in range(4):
        outer = four([turned(inner[q][a], q * a, sign) for q in range(4)], sign)
        for b in range(4):
            out[a + 4 * b] = outer[b]
    return out


def eight(x, sign):
    even, odd = four(x[0::2], sign), four(x[1::2], sign)
    odd = [turned(odd[i], 2 * i, sign) for i in range(4)]
    return [plus(even[i], odd[i]) for i in range(4)] + [minus(even[i], odd[i]) for i in range(4)]


def forward_kernel(k_ref, first_ref, twist_ref, second_ref, o_ref, l_ref):
    for r in range(8):
        row = k_ref[r]
        a = dot(first_ref[...], jnp.concatenate([row, row], axis=0))
        real, imaginary = times((a[:HELD], a[HELD:]), twist_ref[0], twist_ref[1])
        high, low = split(jnp.concatenate([real, imaginary], axis=1))
        l_ref[pl.ds(r * HELD, HELD), :] = jnp.concatenate([high, low, high], axis=1)
    out = dot(l_ref[...], second_ref[...])
    for part in range(2):
        piece = out[:, 128 * part : 128 * part + 128].reshape(8, HELD, 128)
        o_ref[:, part] = jnp.swapaxes(piece, 0, 1)


def whole(shape):
    return pl.BlockSpec(shape, lambda *_: (0,) * len(shape), pipeline_mode=pl.Buffered(1))


def forward(rows, chunk):
    first, twist, second = (jnp.asarray(x) for x in forward_tables(chunk))
    return pl.pallas_call(
        forward_kernel,
        grid=(16,),
        in_specs=[
            pl.BlockSpec((8, None, 64, 256), lambda v: (0, v, 0, 0)),
            whole(first.shape),
            whole(twist.shape),
            whole(second.shape),
        ],
        out_specs=pl.BlockSpec((HELD, 2, 8, 128), lambda v: (0, 0, v, 0)),
        out_shape=jax.ShapeDtypeStruct((HELD, 2, 128, 128), jnp.float32),
        scratch_shapes=[pltpu.VMEM((8 * HELD, 1536), jnp.bfloat16)],
        compiler_params=pltpu.CompilerParams(vmem_limit_bytes=40 << 20),
        cost_estimate=pl.CostEstimate(flops=2 * 128 * HELD * 2500 * 256, bytes_accessed=8 << 20, transcendentals=0),
        name="forward",
    )(rows, first, twist, second)


def filter_rows(z_ref, position, x_ref_twist, waves_ref, squares_ref, s_ref, q_ref):
    group, j = position // 8, position % 8
    for part in range(2):
        rows = pl.ds(pl.multiple_of(group * 16 + part * 8, 8), 8)
        square = squares_ref[rows, :]
        values = []
        for v in range(16):
            x = z_ref[v * 16 + part * 8 : v * 16 + part * 8 + 8, :128], z_ref[v * 16 + part * 8 : v * 16 + part * 8 + 8, 128:]
            if v:
                x = times(x, x_ref_twist[j, 2 * v : 2 * v + 1, :], x_ref_twist[j, 2 * v + 1 : 2 * v + 2, :])
            values.append(x)
        values = sixteen(values, -1)
        q_ref[j, 0, rows, :] = values[8][0] + jnp.where(square == 0.0, values[0][0], 0.0)
        q_ref[j, 1, rows, :] = values[8][1] + jnp.where(square == 0.0, values[0][1], 0.0)
        totals = None
        for a in range(16):
            wave = waves_ref[j, a : a + 1, :]
            below = waves_ref[j, 16 + a : 17 + a, :] + square
            if a == 0:
                scale = jnp.where(below > 0.0, 1.0 / jnp.where(below > 0.0, below, 1.0), 0.0)
            else:
                scale = 1.0 / below
            if a == 8:
                scale = scale * waves_ref[j, 32:33, :]
            real, imaginary = values[a][0] * scale, values[a][1] * scale
            terms = [real, imaginary, real * wave, imaginary * wave]
            totals = terms if totals is None else [p + t for p, t in zip(totals, terms)]
        for f in range(4):
            s_ref[f, j, rows, :] = totals[f]


def row_kernel(x_ref, squares_ref, grid_ref, twist_ref, waves_ref, back_ref, left_ref, o_ref, l_ref, z0_ref, z1_ref, s_ref, q_ref, g_ref, r_ref):
    k = pl.program_id(0)

    def arrange(v, _):
        rows = pl.ds(pl.multiple_of(v * 8, 8), 8)
        real = x_ref[:, 0, rows, :].reshape(128, 128)
        imaginary = x_ref[:, 1, rows, :].reshape(128, 128)
        high, low = split(jnp.concatenate([real.T, imaginary.T], axis=1))
        l_ref[:, v] = jnp.concatenate([high, low, high], axis=1).reshape(8, 16, 768)
        return 0

    lax.fori_loop(0, 16, arrange, 0)

    def multiply(position, z_ref):
        z_ref[...] = dot(l_ref[position // 8].reshape(256, 768), grid_ref[position % 8])

    def filtered(position, z_ref):
        filter_rows(z_ref, position, twist_ref, waves_ref, squares_ref, s_ref, q_ref)

    multiply(0, z0_ref)

    def pair(h, _):
        multiply(2 * h + 1, z1_ref)
        filtered(2 * h, z0_ref)
        multiply(jnp.minimum(2 * h + 2, 63), z0_ref)
        filtered(2 * h + 1, z1_ref)
        return 0

    lax.fori_loop(0, 32, pair, 0)

    def unfold(group, _):
        rows = pl.ds(pl.multiple_of(group * 16, 16), 16)
        for f in range(2):
            values = eight([(s_ref[2 * f, j, rows, :], s_ref[2 * f + 1, j, rows, :]) for j in range(8)], 1)
            for i in range(8):
                real, imaginary = times(values[i], back_ref[2 * i : 2 * i + 1, :], back_ref[2 * i + 1 : 2 * i + 2, :])
                high, low = split(jnp.concatenate([real, imaginary], axis=1))
                g_ref[8 * f + i, rows, :] = jnp.concatenate([high, low, high], axis=1)
        return 0

    lax.fori_loop(0, 8, unfold, 0)

    def outward(q, _):
        for e in range(4):
            result = lax.dot_general(left_ref[...], g_ref[4 * q + e], (((1,), (1,)), ((), ())), preferred_element_type=jnp.float32)
            r_ref[2 * e] = result[:128]
            r_ref[2 * e + 1] = result[128:]
        o_ref[:, pl.ds(pl.multiple_of(k * 32 + q * 8, 8), 8), :] = jnp.swapaxes(r_ref[...], 0, 1)
        return 0

    lax.fori_loop(0, 4, outward, 0)

    @pl.when(k == 0)
    def _():
        o_ref[:, 32 * PER_CHUNK :, :] = jnp.zeros((128, 8, 128), jnp.float32)

    for part in range(2):
        line = q_ref[0, part].T[0:1] * (1.0 / N / N)
        place = lax.broadcasted_iota(jnp.int32, (8, 128), 0) == 2 * k + part
        addend = jnp.where(place, jnp.broadcast_to(line, (8, 128)), 0.0)
        o_ref[:, 32 * PER_CHUNK :, :] += jnp.broadcast_to(addend[None], (128, 8, 128))


def row_stage(arrived, chunk, y, z):
    tables = [jnp.asarray(x) for x in row_tables()]
    tables[3] = lax.dynamic_index_in_dim(tables[3], z, 0, keepdims=False)
    t = 4 * y + PER_CHUNK * chunk + jnp.arange(PER_CHUNK, dtype=jnp.int32)
    wave = STEP * (64 * jnp.arange(128, dtype=jnp.int32)[None, :] + t[:, None]).astype(jnp.float32)
    squares = jnp.broadcast_to((wave * wave)[:, :, None], (PER_CHUNK, 128, 128))
    return pl.pallas_call(
        row_kernel,
        grid=(PER_CHUNK,),
        in_specs=[
            pl.BlockSpec((16, None, 2, 128, 128), lambda k: (0, k, 0, 0, 0)),
            pl.BlockSpec((None, 128, 128), lambda k: (k, 0, 0)),
        ]
        + [whole(x.shape) for x in tables],
        out_specs=whole((128, ROWS, 128)),
        out_shape=jax.ShapeDtypeStruct((128, ROWS, 128), jnp.float32),
        scratch_shapes=[
            pltpu.VMEM((8, 16, 16, 768), jnp.bfloat16),
            pltpu.VMEM((256, 256), jnp.float32),
            pltpu.VMEM((256, 256), jnp.float32),
            pltpu.VMEM((4, 8, 128, 128), jnp.float32),
            pltpu.VMEM((8, 2, 128, 128), jnp.float32),
            pltpu.VMEM((16, 128, 768), jnp.bfloat16),
            pltpu.VMEM((8, 128, 128), jnp.float32),
        ],
        compiler_params=pltpu.CompilerParams(vmem_limit_bytes=56 << 20),
        cost_estimate=pl.CostEstimate(flops=PER_CHUNK * 2 * 49152 * 65536, bytes_accessed=16 << 20, transcendentals=0),
        name="row_stage",
    )(arrived.reshape(16, PER_CHUNK, 2, 128, 128), squares, *tables)


def final_kernel(*refs):
    y_refs, (k_ref, first_ref, twist_ref, second_ref, scales_ref, o_ref, a_ref, b_ref, r_ref, f_ref) = refs[:CHUNKS], refs[CHUNKS:]
    for chunk in range(CHUNKS):
        for k in range(PER_CHUNK):
            place = 16 * (chunk * PER_CHUNK + k)
            for q in range(4):
                block = y_refs[chunk][:, 32 * k + 8 * q : 32 * k + 8 * q + 8, :]
                a_ref[8 * q : 8 * q + 8, place : place + 16, :] = jnp.swapaxes(block, 0, 1)
        block = jnp.swapaxes(y_refs[chunk][:, 32 * PER_CHUNK :, :], 0, 1)
        for k in range(PER_CHUNK):
            place = 16 * (chunk * PER_CHUNK + k)
            for part in range(2):
                a_ref[32 + part, place : place + 16, :] = block[2 * k + part]

    def synthesis(pairs):
        high, low = split(jnp.concatenate([jnp.concatenate(p, axis=1) for p in pairs], axis=0))
        out = dot(jnp.concatenate([high, low, high], axis=1), first_ref[...])
        results = []
        for f in range(len(pairs)):
            x = out[64 * f : 64 * f + 64, :256], out[64 * f : 64 * f + 64, 256:]
            high, low = split(jnp.concatenate(times(x, twist_ref[0], twist_ref[1]), axis=0))
            results.append(dot(second_ref[...], jnp.concatenate([high, low, high], axis=0)))
        return results

    weight = scales_ref[0]
    r_ref[...] = synthesis([(a_ref[32] * weight, a_ref[33] * weight)])[0]
    sign = (1 - 2 * (lax.broadcasted_iota(jnp.int32, (64, 256), 1) % 2)).astype(jnp.float32)

    def ray(i, _):
        base = a_ref[2 * i], a_ref[2 * i + 1]
        slope = a_ref[16 + 2 * i], a_ref[17 + 2 * i]
        one, wave, square = scales_ref[0], scales_ref[1], scales_ref[2]
        alpha_rows, alpha_cols, curve_cols, curve_mixed = synthesis(
            [
                (-slope[1] * one, slope[0] * one),
                (-base[1] * wave, base[0] * wave),
                (-base[0] * square, -base[1] * square),
                (-slope[0] * wave, -slope[1] * wave),
            ]
        )
        kappa = k_ref[i].astype(jnp.float32)
        edge = sign * (jnp.sum(kappa * sign) * (1.0 / N))
        curve_rows = 2.0 * (kappa - edge - r_ref[...]) - curve_cols
        for f, field in enumerate([alpha_rows, alpha_cols, curve_rows, curve_cols, curve_mixed]):
            f_ref[f, i] = field
        return 0

    lax.fori_loop(0, 8, ray, 0)
    for f in range(5):
        for g in range(8):
            block = jnp.swapaxes(f_ref[f, :, 8 * g : 8 * g + 8, :], 0, 1)
            for v in range(8):
                o_ref[f, :, (8 * g + v) * 256 : (8 * g + v) * 256 + 256] = block[v]


def final_stage(returned, rows):
    tables = [jnp.asarray(x) for x in final_tables()]
    return pl.pallas_call(
        final_kernel,
        grid=(1,),
        in_specs=[whole((16, ROWS, 128))] * CHUNKS
        + [pl.BlockSpec((8, None, 64, 256), lambda v: (0, 0, 0, 0))]
        + [whole(x.shape) for x in tables],
        out_specs=whole((5, 8, N)),
        out_shape=jax.ShapeDtypeStruct((5, 8, N), jnp.float32),
        scratch_shapes=[
            pltpu.VMEM((34, 64, 128), jnp.float32),
            pltpu.VMEM((8, 128), jnp.float32),
            pltpu.VMEM((64, 256), jnp.float32),
            pltpu.VMEM((5, 8, 64, 256), jnp.float32),
        ],
        compiler_params=pltpu.CompilerParams(vmem_limit_bytes=40 << 20),
        cost_estimate=pl.CostEstimate(flops=2 * 16384 * 65536, bytes_accessed=8 << 20, transcendentals=0),
        name="final_stage",
    )(*returned, rows, *tables)


def advance_kernel(w_ref, s_ref, f_ref, o_ref):
    w = w_ref[0]
    o_ref[0] = s_ref[0] - w * f_ref[0]
    o_ref[1] = s_ref[1] - w * f_ref[1]
    rows, cols, mixed = w * f_ref[2], w * f_ref[3], w * f_ref[4]
    upper_left, upper_right, lower_left, lower_right = s_ref[2], s_ref[3], s_ref[4], s_ref[5]
    o_ref[2] = upper_left - (rows * upper_left + mixed * lower_left)
    o_ref[3] = upper_right - (rows * upper_right + mixed * lower_right)
    o_ref[4] = lower_left - (mixed * upper_left + cols * lower_left)
    o_ref[5] = lower_right - (mixed * upper_right + cols * lower_right)


def advance(state, fields, weight):
    width = 2048
    return pl.pallas_call(
        advance_kernel,
        grid=(N // width,),
        in_specs=[
            pl.BlockSpec(memory_space=pltpu.SMEM),
            pl.BlockSpec((6, 8, width), lambda p: (0, 0, p)),
            pl.BlockSpec((5, 8, width), lambda p: (0, 0, p)),
        ],
        out_specs=pl.BlockSpec((6, 8, width), lambda p: (0, 0, p)),
        out_shape=jax.ShapeDtypeStruct((6, 8, N), jnp.float32),
        cost_estimate=pl.CostEstimate(flops=22 * 8 * N, bytes_accessed=17 * 8 * N * 4, transcendentals=0),
        name="advance",
    )(weight, state, fields)


def exchanged(value):
    return lax.all_to_all(value, "col", split_axis=0, concat_axis=0, tiled=True)


def body(convergence, lens_weight, rays_in):
    y, z = lax.axis_index("col"), lax.axis_index("row")
    rows = convergence.reshape(8, 16, 64, 256)
    sent, summed, returned = [], [], []
    for chunk in range(CHUNKS):
        sent.append(forward(rows, chunk))
    for chunk in range(CHUNKS):
        arrived = exchanged(sent[chunk])
        partial = row_stage(arrived, chunk, y, z)
        summed.append(lax.psum_scatter(partial, "row", scatter_dimension=0, tiled=True))
    for chunk in range(CHUNKS):
        returned.append(exchanged(summed[chunk]))
    fields = final_stage(returned, rows)
    state = advance(rays_in, fields, lens_weight)
    received = lax.ppermute(state, "shell", [(0, 1)])
    start = jnp.where(lax.axis_index("shell") == 1, received, rays_in)
    return advance(start, fields, lens_weight)[None]


def solution(mesh):
    in_specs = (P("shell", ("row", "col"), None), P("shell"), P(None, ("row", "col"), None))
    out_specs = P("shell", None, ("row", "col"), None)
    return jax.shard_map(body, mesh=mesh, in_specs=in_specs, out_specs=out_specs, check_vma=False)
```

time: 622 us -> 405 us (0.65)
  Pallas kernels: 0 us -> 163 us
  matrix products: 143 us -> 0 us
  waiting for transfers between devices: 283 us -> 152 us
  other arithmetic: 77.1 us -> 3.88 us
  local copies, waits for them, and re-layouts: 81 us -> 24.6 us
  starting transfers between devices: 30.7 us -> 46.8 us
  between operations: 1.63 us -> 14 us
    pallas_call x0 -> x11, Pallas kernels: none -> 163 us  [the longest x4 106 us: row_stage(): pl.pallas_call(row_kernel, grid=(PER_CHUNK,), in_specs=[pl.BlockSpec((16,...]
    all_to_all x2 -> x8, waiting for transfers between devices: 274 us -> 125 us  [exchanged(): return lax.all_to_all(value, 'col', split_axis=0, concat_axis=0, tiled=True)]
    dot_general x28 -> x0, matrix products: 143 us -> none  [the longest x26 130 us: product(): jnp.einsum(form, left, right, precision=HIGHEST, preferred_element_type=j...]
    unnamed x19 -> x0, other arithmetic: 40 us -> none
    another operation x3 -> x0, local copies, waits for them, and re-layouts: 36.3 us -> none  [the longest x1 31.3 us: column_spectrum(): return jnp.stack([real, imaginary]).reshape(2, devices * block, rows_dev)]
    reduce_sum x2 -> x0, other arithmetic: 19.2 us -> none  [the longest x1 9.66 us: ray_rows(): imaginary = imaginary.reshape(fields, block, STRIDE, rays).sum(axis=2).re...]
    all_to_all x2 -> x8, starting transfers between devices: 29.4 us -> 45.3 us  [exchanged(): return lax.all_to_all(value, 'col', split_axis=0, concat_axis=0, tiled=True)]
    reduce_scatter x0 -> x4, waiting for transfers between devices: none -> 15.7 us  [body(): lax.psum_scatter(partial, 'row', scatter_dimension=0, tiled=True)]
  transfers between devices with their start and end apart: 3 -> 13, of which waited for: 3 -> 9; matrix products, arithmetic and copies ran while one was open for 0% -> 1% of each run, Pallas kernels for 0% -> 27%
where the time goes in v1:
time: 405 us; the launch traced here: 404 us
  Pallas kernels  163 us (40%)
  waiting for transfers between devices  152 us (38%)
  starting transfers between devices  46.8 us (12%)
  local copies, waits for them, and re-layouts  24.6 us (6%)
  between operations  14 us (3%)
    all_to_all x8, waiting for transfers between devices, exchanged(): return lax.all_to_all(value, 'col', split_axis=0, concat_axis=0, tiled=True)  125 us
    pallas_call x4, Pallas kernels, row_stage(): pl.pallas_call(row_kernel, grid=(PER_CHUNK,), in_specs=[pl.BlockSpec((16,...  106 us
    all_to_all x8, starting transfers between devices, exchanged(): return lax.all_to_all(value, 'col', split_axis=0, concat_axis=0, tiled=True)  45.3 us
    pallas_call x4, Pallas kernels, forward(): pl.pallas_call(forward_kernel, grid=(16,), in_specs=[pl.BlockSpec((8, Non...  37 us
    unnamed x49, local copies, waits for them, and re-layouts  20.1 us
    reduce_scatter x4, waiting for transfers between devices, body(): lax.psum_scatter(partial, 'row', scatter_dimension=0, tiled=True)  15.7 us
    pallas_call x2, Pallas kernels, advance(): pl.pallas_call(advance_kernel, grid=(N // width,), in_specs=[pl.BlockSpec...  13.6 us
    ppermute x1, waiting for transfers between devices, body(): received = lax.ppermute(state, 'shell', [(0, 1)])  11.4 us
  transfers between devices with their start and end apart: 13, of which 9 were waited for; matrix products, arithmetic and copies ran while one was open for 1% of the time, Pallas kernels for 27%

profile of v1, /device:TPU:1, one launch (start us, length us, event | category | flops | bytes accessed | tf_op | source)
XLA Modules:
  0.0 404.0 jit_solution(7550416963565022653)
XLA Ops:
  6.5 3.5 copy.40
  10.1 9.3 %forward.5 = f32[16,2,128,128]{3,2,1,0:T(8,128)} custom-call(bf16[8,16,64,256]{3,2,1,0:T(8,128)(2,1)S(1)} %bitcast.11, bf16[32,128]{1,0:T(8,128)(2,1)S(1)} %copy-done.18, f32[2,16,256]{2,1,0:T(8,128)S(1)} %copy-done.14, bf16[1536,256]{1,0:T(8,128)(2,1)S(1)} %copy-done.10), custom_call_target="tpu_custom_call" | custom-call | flops 2621440000 | bytes 8388608 | tf_op jit(solution)/shard_map/forward/pallas_call | solution.py:183
  21.3 7.6 %all-to-all-start.2 = ((f32[16,2,128,128]{3,2,1,0:T(8,128)}), f32[16,2,128,128]{3,2,1,0:T(8,128)S(1)}, u32[]{:S(2)}, u32[]{:S(2)}) async-start(f32[16,2,128,128]{3,2,1,0:T(8,128)} %forward.5), calls=%async_computation.3 | async-start | bytes 4194304 | tf_op jit(solution)/shard_map/all_to_all | solution.py:433
  30.2 26.8 %all-to-all-done.2 = f32[16,2,128,128]{3,2,1,0:T(8,128)S(1)} async-done(((f32[16,2,128,128]{3,2,1,0:T(8,128)}), f32[16,2,128,128]{3,2,1,0:T(8,128)S(1)}, u32[]{:S(2)}, u32[]{:S(2)}) %all-to-all-start.2) | async-done | bytes 2097184 | tf_op jit(solution)/shard_map/all_to_all | solution.py:433
  58.4 26.5 %row_stage.5 = f32[128,40,128]{2,1,0:T(8,128)} custom-call(f32[16,1,2,128,128]{4,3,2,1,0:T(8,128)} %bitcast.17, f32[1,128,128]{2,1,0:T(8,128)} %broadcast_in_dim.11.squares_ref, bf16[8,768,256]{2,1,0:T(8,128)(2,1)} %constant.83.clone.grid_ref, f32[8,32,128]{2,1,0:T(8,128)} %constant.84.clone.twist_ref, f32[8,40,128]{2,1,0:T(8,128)} %constant.85.clone.waves_ref, ...), custom_call_target="tpu_custom_call" | custom-call | flops 6442450944 | bytes 16777216 | tf_op jit(solution)/shard_map/row_stage/pallas_call | solution.py:301
  85.7 2.2 copy-done.2
  87.8 9.2 %forward.6 = f32[16,2,128,128]{3,2,1,0:T(8,128)} custom-call(bf16[8,16,64,256]{3,2,1,0:T(8,128)(2,1)S(1)} %bitcast.12, bf16[32,128]{1,0:T(8,128)(2,1)S(1)} %copy-done.17, f32[2,16,256]{2,1,0:T(8,128)S(1)} %copy-done.13, bf16[1536,256]{1,0:T(8,128)(2,1)S(1)} %copy-done.10), custom_call_target="tpu_custom_call" | custom-call | flops 2621440000 | bytes 8388608 | tf_op jit(solution)/shard_map/forward/pallas_call | solution.py:183
  97.1 3.7 all-to-all-start.4
  100.9 25.3 %all-to-all-done.4 = f32[16,2,128,128]{3,2,1,0:T(8,128)S(1)} async-done(((f32[16,2,128,128]{3,2,1,0:T(8,128)}), f32[16,2,128,128]{3,2,1,0:T(8,128)S(1)}, u32[]{:S(2)}, u32[]{:S(2)}) %all-to-all-start.4) | async-done | bytes 2097184 | tf_op jit(solution)/shard_map/all_to_all | solution.py:433
  127.6 26.6 %row_stage.6 = f32[128,40,128]{2,1,0:T(8,128)} custom-call(f32[16,1,2,128,128]{4,3,2,1,0:T(8,128)} %bitcast.19, f32[1,128,128]{2,1,0:T(8,128)} %broadcast_in_dim.12.squares_ref, bf16[8,768,256]{2,1,0:T(8,128)(2,1)} %constant.83.clone.grid_ref, f32[8,32,128]{2,1,0:T(8,128)} %constant.84.clone.twist_ref, f32[8,40,128]{2,1,0:T(8,128)} %constant.85.clone.waves_ref, ...), custom_call_target="tpu_custom_call" | custom-call | flops 6442450944 | bytes 16777216 | tf_op jit(solution)/shard_map/row_stage/pallas_call | solution.py:301
  157.1 9.2 %forward.7 = f32[16,2,128,128]{3,2,1,0:T(8,128)} custom-call(bf16[8,16,64,256]{3,2,1,0:T(8,128)(2,1)S(1)} %bitcast.13, bf16[32,128]{1,0:T(8,128)(2,1)S(1)} %copy-done.16, f32[2,16,256]{2,1,0:T(8,128)S(1)} %copy-done.12, bf16[1536,256]{1,0:T(8,128)(2,1)S(1)} %copy-done.10), custom_call_target="tpu_custom_call" | custom-call | flops 2621440000 | bytes 8388608 | tf_op jit(solution)/shard_map/forward/pallas_call | solution.py:183
  166.3 6.6 %all-to-all-start.6 = ((f32[16,2,128,128]{3,2,1,0:T(8,128)}), f32[16,2,128,128]{3,2,1,0:T(8,128)S(1)}, u32[]{:S(2)}, u32[]{:S(2)}) async-start(f32[16,2,128,128]{3,2,1,0:T(8,128)} %forward.7), calls=%async_computation.9 | async-start | bytes 4194304 | tf_op jit(solution)/shard_map/all_to_all | solution.py:433
  172.9 25.3 %all-to-all-done.6 = f32[16,2,128,128]{3,2,1,0:T(8,128)S(1)} async-done(((f32[16,2,128,128]{3,2,1,0:T(8,128)}), f32[16,2,128,128]{3,2,1,0:T(8,128)S(1)}, u32[]{:S(2)}, u32[]{:S(2)}) %all-to-all-start.6) | async-done | bytes 2097184 | tf_op jit(solution)/shard_map/all_to_all | solution.py:433
  199.6 26.5 %row_stage.7 = f32[128,40,128]{2,1,0:T(8,128)} custom-call(f32[16,1,2,128,128]{4,3,2,1,0:T(8,128)} %bitcast.20, f32[1,128,128]{2,1,0:T(8,128)} %broadcast_in_dim.13.squares_ref, bf16[8,768,256]{2,1,0:T(8,128)(2,1)} %constant.83.clone.grid_ref, f32[8,32,128]{2,1,0:T(8,128)} %constant.84.clone.twist_ref, f32[8,40,128]{2,1,0:T(8,128)} %constant.85.clone.waves_ref, ...), custom_call_target="tpu_custom_call" | custom-call | flops 6442450944 | bytes 16777216 | tf_op jit(solution)/shard_map/row_stage/pallas_call | solution.py:301
  226.9 2.2 copy-done.4
  229.1 9.2 %forward.4 = f32[16,2,128,128]{3,2,1,0:T(8,128)} custom-call(bf16[8,16,64,256]{3,2,1,0:T(8,128)(2,1)S(1)} %bitcast.14, bf16[32,128]{1,0:T(8,128)(2,1)S(1)} %copy-done.15, f32[2,16,256]{2,1,0:T(8,128)S(1)} %copy-done.11, bf16[1536,256]{1,0:T(8,128)(2,1)S(1)} %copy-done.10), custom_call_target="tpu_custom_call" | custom-call | flops 2621440000 | bytes 8388608 | tf_op jit(solution)/shard_map/forward/pallas_call | solution.py:183
  238.3 6.7 %all-to-all-start = ((f32[16,2,128,128]{3,2,1,0:T(8,128)}), f32[16,2,128,128]{3,2,1,0:T(8,128)S(1)}, u32[]{:S(2)}, u32[]{:S(2)}) async-start(f32[16,2,128,128]{3,2,1,0:T(8,128)} %forward.4), calls=%async_computation | async-start | bytes 4194304 | tf_op jit(solution)/shard_map/all_to_all | solution.py:433
  245.0 25.3 %all-to-all-done = f32[16,2,128,128]{3,2,1,0:T(8,128)S(1)} async-done(((f32[16,2,128,128]{3,2,1,0:T(8,128)}), f32[16,2,128,128]{3,2,1,0:T(8,128)S(1)}, u32[]{:S(2)}, u32[]{:S(2)}) %all-to-all-start) | async-done | bytes 2097184 | tf_op jit(solution)/shard_map/all_to_all | solution.py:433
  271.7 26.5 %row_stage.4 = f32[128,40,128]{2,1,0:T(8,128)} custom-call(f32[16,1,2,128,128]{4,3,2,1,0:T(8,128)} %bitcast.18, f32[1,128,128]{2,1,0:T(8,128)} %broadcast_in_dim.10.squares_ref, bf16[8,768,256]{2,1,0:T(8,128)(2,1)} %constant.83.clone.grid_ref, f32[8,32,128]{2,1,0:T(8,128)} %constant.84.clone.twist_ref, f32[8,40,128]{2,1,0:T(8,128)} %constant.85.clone.waves_ref, ...), custom_call_target="tpu_custom_call" | custom-call | flops 6442450944 | bytes 16777216 | tf_op jit(solution)/shard_map/row_stage/pallas_call | solution.py:301
  298.3 6.8 %all-to-all-start.3 = ((f32[16,40,128]{2,1,0:T(8,128)}), f32[16,40,128]{2,1,0:T(8,128)S(1)}, u32[]{:S(2)}, u32[]{:S(2)}) async-start(f32[16,40,128]{2,1,0:T(8,128)} %reduce-scatter.7.cloned.1.call-done), calls=%async_computation.5 | async-start | bytes 655360 | tf_op jit(solution)/shard_map/all_to_all | solution.py:433
  305.2 7.7 %all-to-all-done.3.refs_1_ = f32[16,40,128]{2,1,0:T(8,128)S(1)} async-done(((f32[16,40,128]{2,1,0:T(8,128)}), f32[16,40,128]{2,1,0:T(8,128)S(1)}, u32[]{:S(2)}, u32[]{:S(2)}) %all-to-all-start.3) | async-done | bytes 327712 | tf_op jit(solution)/shard_map/all_to_all | solution.py:433
  312.8 3.5 all-to-all-start.5
  316.4 7.6 %all-to-all-done.5.refs_2_ = f32[16,40,128]{2,1,0:T(8,128)S(1)} async-done(((f32[16,40,128]{2,1,0:T(8,128)}), f32[16,40,128]{2,1,0:T(8,128)S(1)}, u32[]{:S(2)}, u32[]{:S(2)}) %all-to-all-start.5) | async-done | bytes 327712 | tf_op jit(solution)/shard_map/all_to_all | solution.py:433
  324.0 3.8 all-to-all-start.7
  327.8 15.6 %reduce-scatter.5.cloned.1.call-done = f32[16,40,128]{2,1,0:T(8,128)} async-done(((f32[128,40,128]{2,1,0:T(8,128)}), f32[16,40,128]{2,1,0:T(8,128)}) %reduce-scatter.5.cloned.1.call-update) | async-done | bytes 327696 | tf_op jit(solution)/shard_map/reduce_scatter | solution.py:445
  343.4 6.6 %all-to-all-start.1 = ((f32[16,40,128]{2,1,0:T(8,128)}), f32[16,40,128]{2,1,0:T(8,128)S(1)}, u32[]{:S(2)}, u32[]{:S(2)}) async-start(f32[16,40,128]{2,1,0:T(8,128)} %reduce-scatter.5.cloned.1.call-done), calls=%async_computation.2 | async-start | bytes 655360 | tf_op jit(solution)/shard_map/all_to_all | solution.py:433
  350.6 7.0 %all-to-all-done.1.refs_0_ = f32[16,40,128]{2,1,0:T(8,128)S(1)} async-done(((f32[16,40,128]{2,1,0:T(8,128)}), f32[16,40,128]{2,1,0:T(8,128)S(1)}, u32[]{:S(2)}, u32[]{:S(2)}) %all-to-all-start.1) | async-done | bytes 327712 | tf_op jit(solution)/shard_map/all_to_all | solution.py:433
  359.9 5.9 %final_stage.1.f_ref = f32[5,8,16384]{2,1,0:T(8,128)S(1)} custom-call(f32[16,40,128]{2,1,0:T(8,128)S(1)} %all-to-all-done.1.refs_0_, f32[16,40,128]{2,1,0:T(8,128)S(1)} %all-to-all-done.3.refs_1_, f32[16,40,128]{2,1,0:T(8,128)S(1)} %all-to-all-done.5.refs_2_, f32[16,40,128]{2,1,0:T(8,128)S(1)} %all-to-all-done.7.refs_3_, ...), custom_call_target="tpu_custom_call" | custom-call | flops 2147483648 | bytes 8388608 | tf_op jit(solution)/shard_map/final_stage/pallas_call | solution.py:383
  367.4 6.9 %advance.2 = f32[6,8,16384]{2,1,0:T(8,128)} custom-call(f32[1]{0:T(128)S(6)} %copy.41.w_ref, f32[6,8,16384]{2,1,0:T(8,128)} %s_ref.1, f32[5,8,16384]{2,1,0:T(8,128)} %copy-done), custom_call_target="tpu_custom_call" | custom-call | flops 2883584 | bytes 8912896 | tf_op jit(solution)/shard_map/advance/pallas_call | solution.py:417
  375.6 11.4 %collective-permute-done = f32[6,8,16384]{2,1,0:T(8,128)} collective-permute-done((f32[6,8,16384]{2,1,0:T(8,128)}, f32[6,8,16384]{2,1,0:T(8,128)}, u32[]{:S(2)}, u32[]{:S(2)}) %collective-permute-start) | collective-permute-done | bytes 3145760 | tf_op jit(solution)/shard_map/ppermute | solution.py:450
  386.9 3.8 broadcast_select_fusion.s_ref
  390.8 6.7 %advance.3 = f32[6,8,16384]{2,1,0:T(8,128)} custom-call(f32[1]{0:T(128)S(6)} %copy.41.w_ref, f32[6,8,16384]{2,1,0:T(8,128)} %broadcast_select_fusion.s_ref, f32[5,8,16384]{2,1,0:T(8,128)} %copy-done), custom_call_target="tpu_custom_call" | custom-call | flops 2883584 | bytes 8912896 | tf_op jit(solution)/shard_map/advance/pallas_call | solution.py:417
  (68 shorter events, 18.4 us)
Async XLA Ops:
  6.5 3.5 copy-start.10
  6.5 3.5 copy-start.14
  6.5 3.5 copy-start.18
  19.3 2.0 copy-start.1
  21.3 35.7 %all-to-all-start.2 = ((f32[16,2,128,128]{3,2,1,0:T(8,128)}), f32[16,2,128,128]{3,2,1,0:T(8,128)S(1)}, u32[]{:S(2)}, u32[]{:S(2)}) async-start(f32[16,2,128,128]{3,2,1,0:T(8,128)} %forward.5), calls=%async_computation.3 | async-start | bytes 4194304 | tf_op jit(solution)/shard_map/all_to_all | solution.py:433
  28.9 269.4 %reduce-scatter.7.cloned.1.call-start = ((), (), s32[]{:S(2)}) async-start(), calls=%async_computation.13 | async-start | bytes 2949120 | tf_op jit(solution)/shard_map/reduce_scatter | solution.py:445
  57.0 1.3 copy-start.20
  84.9 0.8 copy-start.17
  85.7 2.2 copy-start.2
  97.1 29.1 %all-to-all-start.4 = ((f32[16,2,128,128]{3,2,1,0:T(8,128)}), f32[16,2,128,128]{3,2,1,0:T(8,128)S(1)}, u32[]{:S(2)}, u32[]{:S(2)}) async-start(f32[16,2,128,128]{3,2,1,0:T(8,128)} %forward.6), calls=%async_computation.6 | async-start | bytes 4194304 | tf_op jit(solution)/shard_map/all_to_all | solution.py:433
  100.8 204.3 %reduce-scatter.9.cloned.1.call-start = ((), (), s32[]{:S(2)}) async-start(), calls=%async_computation.14 | async-start | bytes 2949120 | tf_op jit(solution)/shard_map/reduce_scatter | solution.py:445
  126.2 1.3 copy-start.22
  154.9 2.2 copy-start.3
  166.3 32.0 %all-to-all-start.6 = ((f32[16,2,128,128]{3,2,1,0:T(8,128)}), f32[16,2,128,128]{3,2,1,0:T(8,128)S(1)}, u32[]{:S(2)}, u32[]{:S(2)}) async-start(f32[16,2,128,128]{3,2,1,0:T(8,128)} %forward.7), calls=%async_computation.9 | async-start | bytes 4194304 | tf_op jit(solution)/shard_map/all_to_all | solution.py:433
  172.9 143.5 %reduce-scatter.11.cloned.1.call-start = ((), (), s32[]{:S(2)}) async-start(), calls=%async_computation.15 | async-start | bytes 2949120 | tf_op jit(solution)/shard_map/reduce_scatter | solution.py:445
  198.3 1.3 copy-start.23
  226.9 2.2 copy-start.4
  238.3 32.0 %all-to-all-start = ((f32[16,2,128,128]{3,2,1,0:T(8,128)}), f32[16,2,128,128]{3,2,1,0:T(8,128)S(1)}, u32[]{:S(2)}, u32[]{:S(2)}) async-start(f32[16,2,128,128]{3,2,1,0:T(8,128)} %forward.4), calls=%async_computation | async-start | bytes 4194304 | tf_op jit(solution)/shard_map/all_to_all | solution.py:433
  245.0 98.4 %reduce-scatter.5.cloned.1.call-start = ((), (), s32[]{:S(2)}) async-start(), calls=%async_computation.12 | async-start | bytes 2949120 | tf_op jit(solution)/shard_map/reduce_scatter | solution.py:445
  270.3 1.4 copy-start.21
  298.2 59.5 %copy-start.6 = (bf16[768,512]{1,0:T(8,128)(2,1)S(1)}, bf16[768,512]{1,0:T(8,128)(2,1)}, u32[]{:S(2)}) copy-start(bf16[768,512]{1,0:T(8,128)(2,1)} %constant.88.clone.refs_5_) | copy-start | bytes 2359300
  298.2 59.5 %copy-start.7 = (f32[2,64,256]{2,1,0:T(8,128)S(1)}, f32[2,64,256]{2,1,0:T(8,128)}, u32[]{:S(2)}) copy-start(f32[2,64,256]{2,1,0:T(8,128)} %constant.89.clone.refs_6_) | copy-start | bytes 393220
  298.2 59.5 %copy-start.8 = (f32[3,64,128]{2,1,0:T(8,128)S(1)}, f32[3,64,128]{2,1,0:T(8,128)}, u32[]{:S(2)}) copy-start(f32[3,64,128]{2,1,0:T(8,128)} %constant.91.clone.refs_8_) | copy-start | bytes 294916
  298.2 59.5 %copy-start.9 = (bf16[64,384]{1,0:T(8,128)(2,1)S(1)}, bf16[64,384]{1,0:T(8,128)(2,1)}, u32[]{:S(2)}) copy-start(bf16[64,384]{1,0:T(8,128)(2,1)} %constant.90.clone.refs_7_) | copy-start | bytes 147460
  298.3 14.6 %all-to-all-start.3 = ((f32[16,40,128]{2,1,0:T(8,128)}), f32[16,40,128]{2,1,0:T(8,128)S(1)}, u32[]{:S(2)}, u32[]{:S(2)}) async-start(f32[16,40,128]{2,1,0:T(8,128)} %reduce-scatter.7.cloned.1.call-done), calls=%async_computation.5 | async-start | bytes 655360 | tf_op jit(solution)/shard_map/all_to_all | solution.py:433
  312.8 11.2 %all-to-all-start.5 = ((f32[16,40,128]{2,1,0:T(8,128)}), f32[16,40,128]{2,1,0:T(8,128)S(1)}, u32[]{:S(2)}, u32[]{:S(2)}) async-start(f32[16,40,128]{2,1,0:T(8,128)} %reduce-scatter.9.cloned.1.call-done), calls=%async_computation.8 | async-start | bytes 655360 | tf_op jit(solution)/shard_map/all_to_all | solution.py:433
  324.0 19.4 %all-to-all-start.7 = ((f32[16,40,128]{2,1,0:T(8,128)}), f32[16,40,128]{2,1,0:T(8,128)S(1)}, u32[]{:S(2)}, u32[]{:S(2)}) async-start(f32[16,40,128]{2,1,0:T(8,128)} %reduce-scatter.11.cloned.1.call-done), calls=%async_computation.11 | async-start | bytes 655360 | tf_op jit(solution)/shard_map/all_to_all | solution.py:433
  343.4 14.2 %all-to-all-start.1 = ((f32[16,40,128]{2,1,0:T(8,128)}), f32[16,40,128]{2,1,0:T(8,128)S(1)}, u32[]{:S(2)}, u32[]{:S(2)}) async-start(f32[16,40,128]{2,1,0:T(8,128)} %reduce-scatter.5.cloned.1.call-done), calls=%async_computation.2 | async-start | bytes 655360 | tf_op jit(solution)/shard_map/all_to_all | solution.py:433
  357.7 2.2 copy-start.5
  365.8 1.5 copy-start
  367.4 19.6 %copy-start.19 = (f32[6,8,16384]{2,1,0:T(8,128)S(1)}, f32[6,8,16384]{2,1,0:T(8,128)}, u32[]{:S(2)}) copy-start(f32[6,8,16384]{2,1,0:T(8,128)} %s_ref.1) | copy-start | bytes 9437188
  374.3 12.7 %collective-permute-start = (f32[6,8,16384]{2,1,0:T(8,128)}, f32[6,8,16384]{2,1,0:T(8,128)}, u32[]{:S(2)}, u32[]{:S(2)}) collective-permute-start(f32[6,8,16384]{2,1,0:T(8,128)} %advance.2), channel_id=1, source_target_pairs={{0,128},{1,129},{2,130},{3,131},{4,132},{5,133},{6,134},{7,135},{8... | collective-permute-start | bytes 9437192 | tf_op jit(solution)/shard_map/ppermute | solution.py:450
  (5 other events, 3.8 us)
Sparse Core Ops, SparseCore 0:
  85.0 42.1 reduce-scatter.6
  154.3 44.9 reduce-scatter.8
  226.3 45.0 reduce-scatter.10
  298.4 45.0 reduce-scatter.4

commit v2 on v1

--- a/solution.py
+++ b/solution.py
@@ -15,6 +15,7 @@
 PER_CHUNK = 4 // CHUNKS
 HELD = 16 * PER_CHUNK
 ROWS = 32 * PER_CHUNK + 8
+GROUP = 2
 STEP = 2.0 * math.pi / N
 
 
@@ -229,7 +230,8 @@
             s_ref[f, j, rows, :] = totals[f]
 
 
-def row_kernel(x_ref, squares_ref, grid_ref, twist_ref, waves_ref, back_ref, left_ref, o_ref, l_ref, z0_ref, z1_ref, s_ref, q_ref, g_ref, r_ref):
+def row_kernel(x_ref, squares_ref, grid_ref, twist_ref, waves_ref, back_ref, left_ref, *rest):
+    o_ref, l_ref, z0_ref, z1_ref, s_ref, q_ref, g_ref, r_ref = rest[-8:]
     k = pl.program_id(0)
 
     def arrange(v, _):
@@ -292,8 +294,9 @@
         o_ref[:, 32 * PER_CHUNK :, :] += jnp.broadcast_to(addend[None], (128, 8, 128))
 
 
-def row_stage(arrived, chunk, y, z):
+def row_stage(arrived, chunk, y, z, previous):
     tables = [jnp.asarray(x) for x in row_tables()]
+    held, section = [previous] if previous is not None else [], chunk % GROUP
     tables[3] = lax.dynamic_index_in_dim(tables[3], z, 0, keepdims=False)
     t = 4 * y + PER_CHUNK * chunk + jnp.arange(PER_CHUNK, dtype=jnp.int32)
     wave = STEP * (64 * jnp.arange(128, dtype=jnp.int32)[None, :] + t[:, None]).astype(jnp.float32)
@@ -305,9 +308,11 @@
             pl.BlockSpec((16, None, 2, 128, 128), lambda k: (0, k, 0, 0, 0)),
             pl.BlockSpec((None, 128, 128), lambda k: (k, 0, 0)),
         ]
-        + [whole(x.shape) for x in tables],
-        out_specs=whole((128, ROWS, 128)),
-        out_shape=jax.ShapeDtypeStruct((128, ROWS, 128), jnp.float32),
+        + [whole(x.shape) for x in tables]
+        + [pl.BlockSpec(memory_space=pl.ANY)] * len(held),
+        out_specs=pl.BlockSpec((128, ROWS, 128), lambda k: (0, section, 0), pipeline_mode=pl.Buffered(1)),
+        out_shape=jax.ShapeDtypeStruct((128, GROUP * ROWS, 128), jnp.float32),
+        input_output_aliases={7: 0} if held else {},
         scratch_shapes=[
             pltpu.VMEM((8, 16, 16, 768), jnp.bfloat16),
             pltpu.VMEM((256, 256), jnp.float32),
@@ -320,11 +325,13 @@
         compiler_params=pltpu.CompilerParams(vmem_limit_bytes=56 << 20),
         cost_estimate=pl.CostEstimate(flops=PER_CHUNK * 2 * 49152 * 65536, bytes_accessed=16 << 20, transcendentals=0),
         name="row_stage",
-    )(arrived.reshape(16, PER_CHUNK, 2, 128, 128), squares, *tables)
+    )(arrived.reshape(16, PER_CHUNK, 2, 128, 128), squares, *tables, *held)
 
 
 def final_kernel(*refs):
-    y_refs, (k_ref, first_ref, twist_ref, second_ref, scales_ref, o_ref, a_ref, b_ref, r_ref, f_ref) = refs[:CHUNKS], refs[CHUNKS:]
+    count = CHUNKS // GROUP
+    y_refs = [refs[c // GROUP].at[:, pl.ds(c % GROUP * ROWS, ROWS), :] for c in range(CHUNKS)]
+    w_ref, state_ref, k_ref, first_ref, twist_ref, second_ref, scales_ref, o_ref, n_ref, a_ref, r_ref, f_ref = refs[count:]
     for chunk in range(CHUNKS):
         for k in range(PER_CHUNK):
             place = 16 * (chunk * PER_CHUNK + k)
@@ -371,62 +378,80 @@
         return 0
 
     lax.fori_loop(0, 8, ray, 0)
-    for f in range(5):
-        for g in range(8):
-            block = jnp.swapaxes(f_ref[f, :, 8 * g : 8 * g + 8, :], 0, 1)
-            for v in range(8):
-                o_ref[f, :, (8 * g + v) * 256 : (8 * g + v) * 256 + 256] = block[v]
-
-
-def final_stage(returned, rows):
+
+    def emit(g, _):
+        blocks = [jnp.swapaxes(f_ref[f, :, pl.ds(pl.multiple_of(8 * g, 8), 8), :], 0, 1) for f in range(5)]
+        for v in range(8):
+            place = pl.ds(pl.multiple_of((8 * g + v) * 256, 256), 256)
+            fields = [block[v] for block in blocks]
+            for f in range(5):
+                o_ref[f, :, place] = fields[f]
+            for e, value in enumerate(moved([state_ref[e, :, place] for e in range(6)], fields, w_ref[0])):
+                n_ref[e, :, place] = value
+        return 0
+
+    lax.fori_loop(0, 8, emit, 0)
+
+
+def moved(state, fields, w):
+    rows, cols, mixed = w * fields[2], w * fields[3], w * fields[4]
+    upper_left, upper_right, lower_left, lower_right = state[2:]
+    return [
+        state[0] - w * fields[0],
+        state[1] - w * fields[1],
+        upper_left - (rows * upper_left + mixed * lower_left),
+        upper_right - (rows * upper_right + mixed * lower_right),
+        lower_left - (mixed * upper_left + cols * lower_left),
+        lower_right - (mixed * upper_right + cols * lower_right),
+    ]
+
+
+def final_stage(returned, rows, weight, state):
     tables = [jnp.asarray(x) for x in final_tables()]
     return pl.pallas_call(
         final_kernel,
         grid=(1,),
-        in_specs=[whole((16, ROWS, 128))] * CHUNKS
+        in_specs=[whole((16, GROUP * ROWS, 128))] * (CHUNKS // GROUP)
+        + [pl.BlockSpec(memory_space=pltpu.SMEM), whole((6, 8, N))]
         + [pl.BlockSpec((8, None, 64, 256), lambda v: (0, 0, 0, 0))]
         + [whole(x.shape) for x in tables],
-        out_specs=whole((5, 8, N)),
-        out_shape=jax.ShapeDtypeStruct((5, 8, N), jnp.float32),
+        out_specs=[whole((5, 8, N)), whole((6, 8, N))],
+        out_shape=[jax.ShapeDtypeStruct((5, 8, N), jnp.float32), jax.ShapeDtypeStruct((6, 8, N), jnp.float32)],
         scratch_shapes=[
             pltpu.VMEM((34, 64, 128), jnp.float32),
-            pltpu.VMEM((8, 128), jnp.float32),
             pltpu.VMEM((64, 256), jnp.float32),
             pltpu.VMEM((5, 8, 64, 256), jnp.float32),
         ],
         compiler_params=pltpu.CompilerParams(vmem_limit_bytes=40 << 20),
         cost_estimate=pl.CostEstimate(flops=2 * 16384 * 65536, bytes_accessed=8 << 20, transcendentals=0),
         name="final_stage",
-    )(*returned, rows, *tables)
-
-
-def advance_kernel(w_ref, s_ref, f_ref, o_ref):
-    w = w_ref[0]
-    o_ref[0] = s_ref[0] - w * f_ref[0]
-    o_ref[1] = s_ref[1] - w * f_ref[1]
-    rows, cols, mixed = w * f_ref[2], w * f_ref[3], w * f_ref[4]
-    upper_left, upper_right, lower_left, lower_right = s_ref[2], s_ref[3], s_ref[4], s_ref[5]
-    o_ref[2] = upper_left - (rows * upper_left + mixed * lower_left)
-    o_ref[3] = upper_right - (rows * upper_right + mixed * lower_right)
-    o_ref[4] = lower_left - (mixed * upper_left + cols * lower_left)
-    o_ref[5] = lower_right - (mixed * upper_right + cols * lower_right)
-
-
-def advance(state, fields, weight):
+    )(*returned, weight, state, rows, *tables)
+
+
+def advance_kernel(w_ref, second_ref, s_ref, f_ref, n_ref, o_ref):
+    last = second_ref[0] == 1
+    values = moved([s_ref[e] for e in range(6)], [f_ref[f] for f in range(5)], w_ref[0])
+    for e in range(6):
+        o_ref[e] = jnp.where(last, values[e], n_ref[e])
+
+
+def advance(weight, second, received, fields, state):
     width = 2048
     return pl.pallas_call(
         advance_kernel,
         grid=(N // width,),
         in_specs=[
             pl.BlockSpec(memory_space=pltpu.SMEM),
+            pl.BlockSpec(memory_space=pltpu.SMEM),
             pl.BlockSpec((6, 8, width), lambda p: (0, 0, p)),
             pl.BlockSpec((5, 8, width), lambda p: (0, 0, p)),
+            pl.BlockSpec((6, 8, width), lambda p: (0, 0, p)),
         ],
         out_specs=pl.BlockSpec((6, 8, width), lambda p: (0, 0, p)),
         out_shape=jax.ShapeDtypeStruct((6, 8, N), jnp.float32),
-        cost_estimate=pl.CostEstimate(flops=22 * 8 * N, bytes_accessed=17 * 8 * N * 4, transcendentals=0),
+        cost_estimate=pl.CostEstimate(flops=22 * 8 * N, bytes_accessed=23 * 8 * N * 4, transcendentals=0),
         name="advance",
-    )(weight, state, fields)
+    )(weight, second, received, fields, state)
 
 
 def exchanged(value):
@@ -439,17 +464,19 @@
     sent, summed, returned = [], [], []
     for chunk in range(CHUNKS):
         sent.append(forward(rows, chunk))
+    partial = None
     for chunk in range(CHUNKS):
         arrived = exchanged(sent[chunk])
-        partial = row_stage(arrived, chunk, y, z)
-        summed.append(lax.psum_scatter(partial, "row", scatter_dimension=0, tiled=True))
-    for chunk in range(CHUNKS):
-        returned.append(exchanged(summed[chunk]))
-    fields = final_stage(returned, rows)
-    state = advance(rays_in, fields, lens_weight)
+        partial = row_stage(arrived, chunk, y, z, partial)
+        if chunk % GROUP == GROUP - 1:
+            summed.append(lax.psum_scatter(partial, "row", scatter_dimension=0, tiled=True))
+            partial = None
+    for group in range(CHUNKS // GROUP):
+        returned.append(exchanged(summed[group]))
+    fields, state = final_stage(returned, rows, lens_weight, rays_in)
     received = lax.ppermute(state, "shell", [(0, 1)])
-    start = jnp.where(lax.axis_index("shell") == 1, received, rays_in)
-    return advance(start, fields, lens_weight)[None]
+    second = lax.axis_index("shell").astype(jnp.int32).reshape(1)
+    return advance(lens_weight, second, received, fields, state)[None]
 
 
 def solution(mesh):

time: 405 us -> 354 us (0.87)
  waiting for transfers between devices: 152 us -> 115 us
  starting transfers between devices: 46.8 us -> 39.6 us
    all_to_all x8 -> x6, waiting for transfers between devices: 125 us -> 41.4 us  [exchanged(): return lax.all_to_all(value, 'col', split_axis=0, concat_axis=0, tiled=True)]
    reduce_scatter x4 -> x2, waiting for transfers between devices: 15.7 us -> 65.6 us  [body(): lax.psum_scatter(partial, 'row', scatter_dimension=0, tiled=True)]
    all_to_all x8 -> x6, starting transfers between devices: 45.3 us -> 38.2 us  [exchanged(): return lax.all_to_all(value, 'col', split_axis=0, concat_axis=0, tiled=True)]
    pallas_call x2 -> x1, Pallas kernels: 13.6 us -> 7.34 us  [advance(): pl.pallas_call(advance_kernel, grid=(N // width,), in_specs=[pl.BlockSpec...]
    unnamed x49 -> x47, local copies, waits for them, and re-layouts: 20.1 us -> 19 us
  transfers between devices with their start and end apart: 13 -> 9, of which waited for: 9 -> 5; matrix products, arithmetic and copies ran while one was open for 1% -> 1% of each run, Pallas kernels for 27% -> 31%
where the time goes in v2:
time: 354 us; the launch traced here: 352 us
  Pallas kernels  161 us (45%)
  waiting for transfers between devices  115 us (32%)
  starting transfers between devices  39.6 us (11%)
  local copies, waits for them, and re-layouts  23.3 us (7%)
  between operations  14.3 us (4%)
    pallas_call x4, Pallas kernels, row_stage(): pl.pallas_call(row_kernel, grid=(PER_CHUNK,), in_specs=[pl.BlockSpec((16,...  106 us
    reduce_scatter x2, waiting for transfers between devices, body(): lax.psum_scatter(partial, 'row', scatter_dimension=0, tiled=True)  65.6 us
    all_to_all x6, waiting for transfers between devices, exchanged(): return lax.all_to_all(value, 'col', split_axis=0, concat_axis=0, tiled=True)  41.4 us
    all_to_all x6, starting transfers between devices, exchanged(): return lax.all_to_all(value, 'col', split_axis=0, concat_axis=0, tiled=True)  38.2 us
    pallas_call x4, Pallas kernels, forward(): pl.pallas_call(forward_kernel, grid=(16,), in_specs=[pl.BlockSpec((8, Non...  37.3 us
    unnamed x47, local copies, waits for them, and re-layouts  19 us
    pallas_call x1, Pallas kernels, final_stage(): pl.pallas_call(final_kernel, grid=(1,), in_specs=[whole((16, GROUP * ROWS...  9.75 us
    ppermute x1, waiting for transfers between devices, body(): received = lax.ppermute(state, 'shell', [(0, 1)])  7.58 us
  transfers between devices with their start and end apart: 9, of which 5 were waited for; matrix products, arithmetic and copies ran while one was open for 1% of the time, Pallas kernels for 31%

profile of v2, /device:TPU:1, one launch (start us, length us, event | category | flops | bytes accessed | tf_op | source)
XLA Modules:
  0.0 352.5 jit_solution(6149927804388789056)
XLA Ops:
  6.5 3.5 copy.42
  10.1 9.4 %forward.7 = f32[16,2,128,128]{3,2,1,0:T(8,128)} custom-call(bf16[8,16,64,256]{3,2,1,0:T(8,128)(2,1)S(1)} %bitcast.12, bf16[32,128]{1,0:T(8,128)(2,1)S(1)} %copy-done.18, f32[2,16,256]{2,1,0:T(8,128)S(1)} %copy-done.14, bf16[1536,256]{1,0:T(8,128)(2,1)S(1)} %copy-done.10), custom_call_target="tpu_custom_call" | custom-call | flops 2621440000 | bytes 8388608 | tf_op jit(solution)/shard_map/forward/pallas_call | solution.py:184
  19.5 2.0 copy-done
  21.5 7.7 %all-to-all-start.4 = ((f32[16,2,128,128]{3,2,1,0:T(8,128)}), f32[16,2,128,128]{3,2,1,0:T(8,128)S(1)}, u32[]{:S(2)}, u32[]{:S(2)}) async-start(f32[16,2,128,128]{3,2,1,0:T(8,128)} %forward.7), calls=%async_computation.5 | async-start | bytes 4194304 | tf_op jit(solution)/shard_map/all_to_all | solution.py:458
  29.3 2.2 copy-done.1
  31.5 9.2 %forward.6 = f32[16,2,128,128]{3,2,1,0:T(8,128)} custom-call(bf16[8,16,64,256]{3,2,1,0:T(8,128)(2,1)S(1)} %bitcast.14, bf16[32,128]{1,0:T(8,128)(2,1)S(1)} %copy-done.17, f32[2,16,256]{2,1,0:T(8,128)S(1)} %copy-done.13, bf16[1536,256]{1,0:T(8,128)(2,1)S(1)} %copy-done.10), custom_call_target="tpu_custom_call" | custom-call | flops 2621440000 | bytes 8388608 | tf_op jit(solution)/shard_map/forward/pallas_call | solution.py:184
  40.7 16.7 %all-to-all-done.4 = f32[16,2,128,128]{3,2,1,0:T(8,128)S(1)} async-done(((f32[16,2,128,128]{3,2,1,0:T(8,128)}), f32[16,2,128,128]{3,2,1,0:T(8,128)S(1)}, u32[]{:S(2)}, u32[]{:S(2)}) %all-to-all-start.4) | async-done | bytes 2097184 | tf_op jit(solution)/shard_map/all_to_all | solution.py:458
  57.4 4.4 %all-to-all-start.3 = ((f32[16,2,128,128]{3,2,1,0:T(8,128)}), f32[16,2,128,128]{3,2,1,0:T(8,128)}, u32[]{:S(2)}, u32[]{:S(2)}) async-start(f32[16,2,128,128]{3,2,1,0:T(8,128)} %forward.6), calls=%async_computation.4 | async-start | bytes 4194304 | tf_op jit(solution)/shard_map/all_to_all | solution.py:458
  61.9 1.3 dynamic-slice_bitcast_fusion.back_ref
  63.9 26.6 %row_stage.6.rest_0_ = f32[128,80,128]{2,1,0:T(8,128)} custom-call(f32[16,1,2,128,128]{4,3,2,1,0:T(8,128)} %bitcast.18, f32[1,128,128]{2,1,0:T(8,128)} %broadcast_in_dim.13.squares_ref, bf16[8,768,256]{2,1,0:T(8,128)(2,1)} %constant.83.clone.grid_ref, f32[8,32,128]{2,1,0:T(8,128)} %constant.84.clone.twist_ref, f32[8,40,128]{2,1,0:T(8,128)} %constant.85.clone.waves_ref, ...), custom_call_target="tpu_custom_call" | custom-call | flops 6442450944 | bytes 16777216 | tf_op jit(solution)/shard_map/row_stage/pallas_call | solution.py:304
  91.3 26.6 %row_stage.7 = f32[128,80,128]{2,1,0:T(8,128)} custom-call(f32[16,1,2,128,128]{4,3,2,1,0:T(8,128)} %bitcast.4.x_ref, f32[1,128,128]{2,1,0:T(8,128)} %broadcast_in_dim.12.squares_ref, bf16[8,768,256]{2,1,0:T(8,128)(2,1)} %constant.83.clone.grid_ref, f32[8,32,128]{2,1,0:T(8,128)} %constant.84.clone.twist_ref, ...), custom_call_target="tpu_custom_call", output_to_operand_aliasing={{}: (7, {})} | custom-call | flops 6442450944 | bytes 16777216 | tf_op jit(solution)/shard_map/row_stage/pallas_call | solution.py:304
  118.6 2.2 copy-done.2
  120.8 9.4 %forward.5 = f32[16,2,128,128]{3,2,1,0:T(8,128)} custom-call(bf16[8,16,64,256]{3,2,1,0:T(8,128)(2,1)S(1)} %bitcast.15, bf16[32,128]{1,0:T(8,128)(2,1)S(1)} %copy-done.16, f32[2,16,256]{2,1,0:T(8,128)S(1)} %copy-done.12, bf16[1536,256]{1,0:T(8,128)(2,1)S(1)} %copy-done.10), custom_call_target="tpu_custom_call" | custom-call | flops 2621440000 | bytes 8388608 | tf_op jit(solution)/shard_map/forward/pallas_call | solution.py:184
  130.2 6.7 %all-to-all-start.1 = ((f32[16,2,128,128]{3,2,1,0:T(8,128)}), f32[16,2,128,128]{3,2,1,0:T(8,128)S(1)}, u32[]{:S(2)}, u32[]{:S(2)}) async-start(f32[16,2,128,128]{3,2,1,0:T(8,128)} %forward.5), calls=%async_computation.1 | async-start | bytes 4194304 | tf_op jit(solution)/shard_map/all_to_all | solution.py:458
  136.9 2.2 copy-done.3
  139.1 9.2 %forward.4 = f32[16,2,128,128]{3,2,1,0:T(8,128)} custom-call(bf16[8,16,64,256]{3,2,1,0:T(8,128)(2,1)S(1)} %bitcast.16, bf16[32,128]{1,0:T(8,128)(2,1)S(1)} %copy-done.15, f32[2,16,256]{2,1,0:T(8,128)S(1)} %copy-done.11, bf16[1536,256]{1,0:T(8,128)(2,1)S(1)} %copy-done.10), custom_call_target="tpu_custom_call" | custom-call | flops 2621440000 | bytes 8388608 | tf_op jit(solution)/shard_map/forward/pallas_call | solution.py:184
  148.3 13.7 %all-to-all-done.1 = f32[16,2,128,128]{3,2,1,0:T(8,128)S(1)} async-done(((f32[16,2,128,128]{3,2,1,0:T(8,128)}), f32[16,2,128,128]{3,2,1,0:T(8,128)S(1)}, u32[]{:S(2)}, u32[]{:S(2)}) %all-to-all-start.1) | async-done | bytes 2097184 | tf_op jit(solution)/shard_map/all_to_all | solution.py:458
  162.0 1.3 copy-done.22
  163.3 5.8 %all-to-all-start = ((f32[16,2,128,128]{3,2,1,0:T(8,128)}), f32[16,2,128,128]{3,2,1,0:T(8,128)S(1)}, u32[]{:S(2)}, u32[]{:S(2)}) async-start(f32[16,2,128,128]{3,2,1,0:T(8,128)} %forward.4), calls=%async_computation | async-start | bytes 4194304 | tf_op jit(solution)/shard_map/all_to_all | solution.py:458
  169.9 26.6 %row_stage.4.rest_0_ = f32[128,80,128]{2,1,0:T(8,128)} custom-call(f32[16,1,2,128,128]{4,3,2,1,0:T(8,128)} %bitcast.20, f32[1,128,128]{2,1,0:T(8,128)} %broadcast_in_dim.11.squares_ref, bf16[8,768,256]{2,1,0:T(8,128)(2,1)} %constant.83.clone.grid_ref, f32[8,32,128]{2,1,0:T(8,128)} %constant.84.clone.twist_ref, f32[8,40,128]{2,1,0:T(8,128)} %constant.85.clone.waves_ref, ...), custom_call_target="tpu_custom_call" | custom-call | flops 6442450944 | bytes 16777216 | tf_op jit(solution)/shard_map/row_stage/pallas_call | solution.py:304
  197.8 26.6 %row_stage.5 = f32[128,80,128]{2,1,0:T(8,128)} custom-call(f32[16,1,2,128,128]{4,3,2,1,0:T(8,128)} %bitcast.19, f32[1,128,128]{2,1,0:T(8,128)} %broadcast_in_dim.10.squares_ref, bf16[8,768,256]{2,1,0:T(8,128)(2,1)} %constant.83.clone.grid_ref, f32[8,32,128]{2,1,0:T(8,128)} %constant.84.clone.twist_ref, ...), custom_call_target="tpu_custom_call", output_to_operand_aliasing={{}: (7, {})} | custom-call | flops 6442450944 | bytes 16777216 | tf_op jit(solution)/shard_map/row_stage/pallas_call | solution.py:304
  224.5 7.0 %all-to-all-start.5 = ((f32[16,80,128]{2,1,0:T(8,128)}), f32[16,80,128]{2,1,0:T(8,128)}, u32[]{:S(2)}, u32[]{:S(2)}) async-start(f32[16,80,128]{2,1,0:T(8,128)} %reduce-scatter.5.cloned.1.call-done), calls=%async_computation.7 | async-start | bytes 1310720 | tf_op jit(solution)/shard_map/all_to_all | solution.py:458
  231.4 65.6 %reduce-scatter.3.cloned.1.call-done = f32[16,80,128]{2,1,0:T(8,128)} async-done(((f32[128,80,128]{2,1,0:T(8,128)}), f32[16,80,128]{2,1,0:T(8,128)}) %reduce-scatter.3.cloned.1.call-update) | async-done | bytes 655376 | tf_op jit(solution)/shard_map/reduce_scatter | solution.py:472
  297.0 6.6 %all-to-all-start.2 = ((f32[16,80,128]{2,1,0:T(8,128)}), f32[16,80,128]{2,1,0:T(8,128)}, u32[]{:S(2)}, u32[]{:S(2)}) async-start(f32[16,80,128]{2,1,0:T(8,128)} %reduce-scatter.3.cloned.1.call-done), calls=%async_computation.3 | async-start | bytes 1310720 | tf_op jit(solution)/shard_map/all_to_all | solution.py:458
  304.3 11.0 %all-to-all-done.2.refs_0_ = f32[16,80,128]{2,1,0:T(8,128)} async-done(((f32[16,80,128]{2,1,0:T(8,128)}), f32[16,80,128]{2,1,0:T(8,128)}, u32[]{:S(2)}, u32[]{:S(2)}) %all-to-all-start.2) | async-done | bytes 655392 | tf_op jit(solution)/shard_map/all_to_all | solution.py:458
  315.3 1.1 copy-done.6
  316.5 9.7 %final_stage.1 = (f32[5,8,16384]{2,1,0:T(8,128)S(1)}, f32[6,8,16384]{2,1,0:T(8,128)}) custom-call(f32[16,80,128]{2,1,0:T(8,128)} %all-to-all-done.2.refs_0_, f32[16,80,128]{2,1,0:T(8,128)} %all-to-all-done.5.refs_1_, f32[1]{0:T(128)S(6)} %copy.45.refs_2_.w_ref, f32[6,8,16384]{2,1,0:T(8,128)S(1)} %copy-done.4, bf16[8,16,64,256]{3,2,1,0:T(8,128)(2,1)} %bitcast.13, ...), custom_call_target="tpu_custom_call" | custom-call | flops 2147483648 | bytes 8388608 | tf_op jit(solution)/shard_map/final_stage/pallas_call | solution.py:411
  326.2 1.5 copy-done.5
  327.7 1.3 collective-permute-start
  329.0 7.6 %collective-permute-done.s_ref = f32[6,8,16384]{2,1,0:T(8,128)S(1)} collective-permute-done((f32[6,8,16384]{2,1,0:T(8,128)}, f32[6,8,16384]{2,1,0:T(8,128)S(1)}, u32[]{:S(2)}, u32[]{:S(2)}) %collective-permute-start) | collective-permute-done | bytes 3145760 | tf_op jit(solution)/shard_map/ppermute | solution.py:477
  336.6 1.7 copy-done.19
  338.3 7.3 %advance.1 = f32[6,8,16384]{2,1,0:T(8,128)} custom-call(f32[1]{0:T(128)S(6)} %copy.45.refs_2_.w_ref, s32[1]{0:T(128)} %bitcast.second_ref, f32[6,8,16384]{2,1,0:T(8,128)} %copy-done.19, f32[5,8,16384]{2,1,0:T(8,128)} %copy-done.5, f32[6,8,16384]{2,1,0:T(8,128)} %get-tuple-element.7.n_ref), custom_call_target="tpu_custom_call" | custom-call | flops 2883584 | bytes 12058624 | tf_op jit(solution)/shard_map/advance/pallas_call | solution.py:440
  (54 shorter events, 4.4 us)
Async XLA Ops:
  6.5 3.5 copy-start.10
  6.5 3.5 copy-start.14
  6.5 3.5 copy-start.18
  19.5 2.0 copy-start
  21.5 7.7 %copy-start.13 = (f32[2,16,256]{2,1,0:T(8,128)S(1)}, f32[2,16,256]{2,1,0:T(8,128)}, u32[]{:S(2)}) copy-start(f32[2,16,256]{2,1,0:T(8,128)} %constant.82.clone.twist_ref) | copy-start | bytes 98308
  21.5 7.7 %copy-start.17 = (bf16[32,128]{1,0:T(8,128)(2,1)S(1)}, bf16[32,128]{1,0:T(8,128)(2,1)}, u32[]{:S(2)}) copy-start(bf16[32,128]{1,0:T(8,128)(2,1)} %constant.81.clone.first_ref) | copy-start | bytes 24580
  21.5 35.9 %all-to-all-start.4 = ((f32[16,2,128,128]{3,2,1,0:T(8,128)}), f32[16,2,128,128]{3,2,1,0:T(8,128)S(1)}, u32[]{:S(2)}, u32[]{:S(2)}) async-start(f32[16,2,128,128]{3,2,1,0:T(8,128)} %forward.7), calls=%async_computation.5 | async-start | bytes 4194304 | tf_op jit(solution)/shard_map/all_to_all | solution.py:458
  29.3 2.2 copy-start.1
  57.4 6.5 %copy-start.20 = (f32[16,2,128,128]{3,2,1,0:T(8,128)}, f32[16,2,128,128]{3,2,1,0:T(8,128)S(1)}, u32[]{:S(2)}) copy-start(f32[16,2,128,128]{3,2,1,0:T(8,128)S(1)} %all-to-all-done.4) | copy-start | bytes 6291460
  57.4 33.2 %all-to-all-start.3 = ((f32[16,2,128,128]{3,2,1,0:T(8,128)}), f32[16,2,128,128]{3,2,1,0:T(8,128)}, u32[]{:S(2)}, u32[]{:S(2)}) async-start(f32[16,2,128,128]{3,2,1,0:T(8,128)} %forward.6), calls=%async_computation.4 | async-start | bytes 4194304 | tf_op jit(solution)/shard_map/all_to_all | solution.py:458
  61.8 162.6 %reduce-scatter.5.cloned.1.call-start = ((), (), s32[]{:S(2)}) async-start(), calls=%async_computation.9 | async-start | bytes 5898240 | tf_op jit(solution)/shard_map/reduce_scatter | solution.py:472
  117.8 0.8 copy-start.12
  117.8 0.8 copy-start.16
  118.6 2.2 copy-start.2
  130.2 6.7 %copy-start.11 = (f32[2,16,256]{2,1,0:T(8,128)S(1)}, f32[2,16,256]{2,1,0:T(8,128)}, u32[]{:S(2)}) copy-start(f32[2,16,256]{2,1,0:T(8,128)} %constant.78.clone.twist_ref) | copy-start | bytes 98308
  130.2 6.7 %copy-start.15 = (bf16[32,128]{1,0:T(8,128)(2,1)S(1)}, bf16[32,128]{1,0:T(8,128)(2,1)}, u32[]{:S(2)}) copy-start(bf16[32,128]{1,0:T(8,128)(2,1)} %constant.77.clone.first_ref) | copy-start | bytes 24580
  130.2 31.8 %all-to-all-start.1 = ((f32[16,2,128,128]{3,2,1,0:T(8,128)}), f32[16,2,128,128]{3,2,1,0:T(8,128)S(1)}, u32[]{:S(2)}, u32[]{:S(2)}) async-start(f32[16,2,128,128]{3,2,1,0:T(8,128)} %forward.5), calls=%async_computation.1 | async-start | bytes 4194304 | tf_op jit(solution)/shard_map/all_to_all | solution.py:458
  136.9 2.2 copy-start.3
  162.0 1.3 copy-start.22
  163.3 33.2 %all-to-all-start = ((f32[16,2,128,128]{3,2,1,0:T(8,128)}), f32[16,2,128,128]{3,2,1,0:T(8,128)S(1)}, u32[]{:S(2)}, u32[]{:S(2)}) async-start(f32[16,2,128,128]{3,2,1,0:T(8,128)} %forward.4), calls=%async_computation | async-start | bytes 4194304 | tf_op jit(solution)/shard_map/all_to_all | solution.py:458
  169.1 127.9 %reduce-scatter.3.cloned.1.call-start = ((), (), s32[]{:S(2)}) async-start(), calls=%async_computation.8 | async-start | bytes 5898240 | tf_op jit(solution)/shard_map/reduce_scatter | solution.py:472
  196.5 1.3 copy-start.21
  224.4 90.9 %copy-start.4 = (f32[6,8,16384]{2,1,0:T(8,128)S(1)}, f32[6,8,16384]{2,1,0:T(8,128)}, u32[]{:S(2)}) copy-start(f32[6,8,16384]{2,1,0:T(8,128)} %refs_3_.1) | copy-start | bytes 9437188
  224.4 90.9 %copy-start.7 = (f32[2,64,256]{2,1,0:T(8,128)S(1)}, f32[2,64,256]{2,1,0:T(8,128)}, u32[]{:S(2)}) copy-start(f32[2,64,256]{2,1,0:T(8,128)} %constant.89.clone.refs_6_) | copy-start | bytes 393220
  224.4 90.9 %copy-start.8 = (f32[3,64,128]{2,1,0:T(8,128)S(1)}, f32[3,64,128]{2,1,0:T(8,128)}, u32[]{:S(2)}) copy-start(f32[3,64,128]{2,1,0:T(8,128)} %constant.91.clone.refs_8_) | copy-start | bytes 294916
  224.4 90.9 %copy-start.9 = (bf16[64,384]{1,0:T(8,128)(2,1)S(1)}, bf16[64,384]{1,0:T(8,128)(2,1)}, u32[]{:S(2)}) copy-start(bf16[64,384]{1,0:T(8,128)(2,1)} %constant.90.clone.refs_7_) | copy-start | bytes 147460
  224.5 72.6 %all-to-all-start.5 = ((f32[16,80,128]{2,1,0:T(8,128)}), f32[16,80,128]{2,1,0:T(8,128)}, u32[]{:S(2)}, u32[]{:S(2)}) async-start(f32[16,80,128]{2,1,0:T(8,128)} %reduce-scatter.5.cloned.1.call-done), calls=%async_computation.7 | async-start | bytes 1310720 | tf_op jit(solution)/shard_map/all_to_all | solution.py:458
  297.0 18.3 %all-to-all-start.2 = ((f32[16,80,128]{2,1,0:T(8,128)}), f32[16,80,128]{2,1,0:T(8,128)}, u32[]{:S(2)}, u32[]{:S(2)}) async-start(f32[16,80,128]{2,1,0:T(8,128)} %reduce-scatter.3.cloned.1.call-done), calls=%async_computation.3 | async-start | bytes 1310720 | tf_op jit(solution)/shard_map/all_to_all | solution.py:458
  315.3 1.1 copy-start.6
  326.2 1.5 copy-start.5
  327.7 8.9 %collective-permute-start = (f32[6,8,16384]{2,1,0:T(8,128)}, f32[6,8,16384]{2,1,0:T(8,128)S(1)}, u32[]{:S(2)}, u32[]{:S(2)}) collective-permute-start(f32[6,8,16384]{2,1,0:T(8,128)} %get-tuple-element.7.n_ref), channel_id=1, source_target_pairs={{0,128},{1,129},{2,130},{3,131},{4,132},{5,133},{6,134},{7,135},{8... | collective-permute-start | bytes 9437192 | tf_op jit(solution)/shard_map/ppermute | solution.py:477
  336.6 1.7 copy-start.19
Sparse Core Ops, SparseCore 0:
  118.0 70.7 reduce-scatter.4
  224.6 72.4 reduce-scatter.2

commit v3 on v2

--- a/solution.py
+++ b/solution.py
@@ -1,3 +1,4 @@
+import functools
 import math
 
 import jax
@@ -9,13 +10,13 @@
 from jax.experimental.pallas import tpu as pltpu
 from jax.sharding import PartitionSpec as P
 
-
 N = 16384
 CHUNKS = 4
-PER_CHUNK = 4 // CHUNKS
-HELD = 16 * PER_CHUNK
-ROWS = 32 * PER_CHUNK + 8
-GROUP = 2
+HELD = 16 * CHUNKS
+ROWS = 40
+COLS = 16
+DEEP = 8
+LANES = 4
 STEP = 2.0 * math.pi / N
 
 
@@ -47,12 +48,8 @@
     return np.block([[cosine, sine], [-sine, cosine]])
 
 
-def bins_of(chunk):
-    return np.array([4 * y + PER_CHUNK * chunk + k for y in range(16) for k in range(PER_CHUNK)])
-
-
-def forward_tables(chunk):
-    t = bins_of(chunk)
+def forward_tables():
+    t = np.array([4 * y + k for k in range(CHUNKS) for y in range(COLS)])
     cosine, sine = turns(t, np.arange(64), 64, -1)
     high, low = halves(np.concatenate([cosine, sine], axis=0))
     first = np.concatenate([high, low], axis=1)
@@ -179,8 +176,8 @@
     return pl.BlockSpec(shape, lambda *_: (0,) * len(shape), pipeline_mode=pl.Buffered(1))
 
 
-def forward(rows, chunk):
-    first, twist, second = (jnp.asarray(x) for x in forward_tables(chunk))
+def forward(rows):
+    first, twist, second = (jnp.asarray(x) for x in forward_tables())
     return pl.pallas_call(
         forward_kernel,
         grid=(16,),
@@ -230,10 +227,7 @@
             s_ref[f, j, rows, :] = totals[f]
 
 
-def row_kernel(x_ref, squares_ref, grid_ref, twist_ref, waves_ref, back_ref, left_ref, *rest):
-    o_ref, l_ref, z0_ref, z1_ref, s_ref, q_ref, g_ref, r_ref = rest[-8:]
-    k = pl.program_id(0)
-
+def row_chunk(x_ref, squares_ref, grid_ref, twist_ref, waves_ref, back_ref, left_ref, o_ref, l_ref, z0_ref, z1_ref, s_ref, q_ref, g_ref, r_ref, between):
     def arrange(v, _):
         rows = pl.ds(pl.multiple_of(v * 8, 8), 8)
         real = x_ref[:, 0, rows, :].reshape(128, 128)
@@ -259,7 +253,13 @@
         filtered(2 * h + 1, z1_ref)
         return 0
 
-    lax.fori_loop(0, 32, pair, 0)
+    def segment(g, _):
+        lax.fori_loop(0, 4, lambda h, c: pair(4 * g + h, c), 0)
+        between(g)
+        return 0
+
+    lax.fori_loop(0, 7, segment, 0)
+    lax.fori_loop(28, 32, pair, 0)
 
     def unfold(group, _):
         rows = pl.ds(pl.multiple_of(group * 16, 16), 16)
@@ -278,42 +278,182 @@
             result = lax.dot_general(left_ref[...], g_ref[4 * q + e], (((1,), (1,)), ((), ())), preferred_element_type=jnp.float32)
             r_ref[2 * e] = result[:128]
             r_ref[2 * e + 1] = result[128:]
-        o_ref[:, pl.ds(pl.multiple_of(k * 32 + q * 8, 8), 8), :] = jnp.swapaxes(r_ref[...], 0, 1)
+        o_ref[:, pl.ds(pl.multiple_of(q * 8, 8), 8), :] = jnp.swapaxes(r_ref[...], 0, 1)
         return 0
 
     lax.fori_loop(0, 4, outward, 0)
-
-    @pl.when(k == 0)
-    def _():
-        o_ref[:, 32 * PER_CHUNK :, :] = jnp.zeros((128, 8, 128), jnp.float32)
-
+    lines = jnp.zeros((8, 128), jnp.float32)
     for part in range(2):
         line = q_ref[0, part].T[0:1] * (1.0 / N / N)
-        place = lax.broadcasted_iota(jnp.int32, (8, 128), 0) == 2 * k + part
-        addend = jnp.where(place, jnp.broadcast_to(line, (8, 128)), 0.0)
-        o_ref[:, 32 * PER_CHUNK :, :] += jnp.broadcast_to(addend[None], (128, 8, 128))
-
-
-def row_stage(arrived, chunk, y, z, previous):
+        place = lax.broadcasted_iota(jnp.int32, (8, 128), 0) == part
+        lines = lines + jnp.where(place, jnp.broadcast_to(line, (8, 128)), 0.0)
+    o_ref[:, 32:40, :] = jnp.broadcast_to(lines[None], (128, 8, 128))
+
+
+def exchange_kernel(
+    sent_ref, squares_ref, grid_ref, twist_ref, waves_ref, back_ref, left_ref, o_ref,
+    arrived_ref, partial_ref, slot_ref, reduced_ref, landed_ref, l_ref, z0_ref, z1_ref, s_ref, q_ref, g_ref, r_ref,
+    own_sem, in_send, in_recv, ring_send, ring_recv, back_send, back_recv,
+):
+    y, z = lax.axis_index("col"), lax.axis_index("row")
+    right, left = lax.rem(z + 1, DEEP), lax.rem(z + DEEP - 1, DEEP)
+    barrier = pltpu.get_barrier_semaphore()
+
+    def greet(d, _):
+        pl.semaphore_signal(barrier, inc=1, device_id={"col": lax.rem(y + d, COLS)}, device_id_type=pl.DeviceIdType.MESH)
+        return 0
+
+    lax.fori_loop(1, COLS, greet, 0)
+    for neighbour in (left, right):
+        pl.semaphore_signal(barrier, inc=1, device_id={"row": neighbour}, device_id_type=pl.DeviceIdType.MESH)
+    pl.semaphore_wait(barrier, COLS + 1)
+
+    def inward(k, d):
+        peer = lax.rem(y + d, COLS)
+        return pltpu.make_async_remote_copy(
+            sent_ref.at[k, peer], arrived_ref.at[k, y], in_send.at[k, d], in_recv.at[k, d],
+            device_id={"col": peer}, device_id_type=pl.DeviceIdType.MESH,
+        )
+
+    def own(k):
+        return pltpu.make_async_copy(sent_ref.at[k, y], arrived_ref.at[k, y], own_sem.at[k])
+
+    def homeward(k, d):
+        peer = lax.rem(y + d, COLS)
+        rows = pl.ds(pl.multiple_of(k * ROWS, 8), ROWS)
+        return pltpu.make_async_remote_copy(
+            reduced_ref.at[k, peer], landed_ref.at[y, rows], back_send.at[k, d], back_recv.at[k, d],
+            device_id={"col": peer}, device_id_type=pl.DeviceIdType.MESH,
+        )
+
+    def share(block, lane):
+        return pl.ds(lax.rem(block + 2 * DEEP, DEEP) * COLS + 4 * lane, 4)
+
+    def ring(k, lane, s, source):
+        return pltpu.make_async_remote_copy(
+            source, slot_ref.at[k, lane, s], ring_send.at[k, lane, s], ring_recv.at[k, lane, s],
+            device_id={"row": right if lane % 2 == 0 else left}, device_id_type=pl.DeviceIdType.MESH,
+        )
+
+    def open_ring(k):
+        for lane in range(LANES):
+            block = z - 1 if lane % 2 == 0 else z + 1
+            ring(k, lane, 0, partial_ref.at[k, share(block, lane)]).start()
+
+    def step(k, s):
+        for lane in range(LANES):
+            ring(k, lane, s, slot_ref.at[k, lane, s]).wait_recv()
+            block = z - s - 2 if lane % 2 == 0 else z + s + 2
+            total = slot_ref[k, lane, s] + partial_ref[k, share(block, lane)]
+
+            @pl.when(s < DEEP - 2)
+            def _():
+                slot_ref[k, lane, s] = total
+                ring(k, lane, s + 1, slot_ref.at[k, lane, s]).start()
+
+            @pl.when(s == DEEP - 2)
+            def _():
+                reduced_ref[k, 4 * lane : 4 * lane + 4] = total
+
+    def close_ring(k):
+        landed_ref[y, pl.ds(pl.multiple_of(k * ROWS, 8), ROWS), :] = reduced_ref[k, y]
+
+        def give(d, _):
+            homeward(k, d).start()
+            return 0
+
+        lax.fori_loop(1, COLS, give, 0)
+
+    def launch(k, _):
+        own(k).start()
+
+        def give(d, _):
+            inward(k, d).start()
+            return 0
+
+        lax.fori_loop(1, COLS, give, 0)
+        return 0
+
+    lax.fori_loop(0, CHUNKS, launch, 0)
+
+    def chunk(k, _):
+        own(k).wait()
+
+        def take(d, _):
+            inward(k, d).wait_recv()
+            return 0
+
+        lax.fori_loop(1, COLS, take, 0)
+
+        @pl.when(k > 0)
+        def _():
+            open_ring(k - 1)
+
+        def between(s):
+            @pl.when(k > 0)
+            def _():
+                step(k - 1, s)
+
+        row_chunk(
+            arrived_ref.at[k], squares_ref.at[k], grid_ref, twist_ref, waves_ref, back_ref, left_ref,
+            partial_ref.at[k], l_ref, z0_ref, z1_ref, s_ref, q_ref, g_ref, r_ref, between,
+        )
+
+        @pl.when(k > 0)
+        def _():
+            close_ring(k - 1)
+
+        return 0
+
+    lax.fori_loop(0, CHUNKS, chunk, 0)
+    open_ring(CHUNKS - 1)
+
+    def last(s, _):
+        step(CHUNKS - 1, s)
+        return 0
+
+    lax.fori_loop(0, DEEP - 1, last, 0)
+    close_ring(CHUNKS - 1)
+
+    def settle(k, _):
+        def one(d, _):
+            inward(k, d).wait_send()
+            homeward(k, d).wait_send()
+            homeward(k, d).wait_recv()
+            return 0
+
+        lax.fori_loop(1, COLS, one, 0)
+
+        def two(s, _):
+            for lane in range(LANES):
+                ring(k, lane, s, slot_ref.at[k, lane, s]).wait_send()
+            return 0
+
+        lax.fori_loop(0, DEEP - 1, two, 0)
+        return 0
+
+    lax.fori_loop(0, CHUNKS, settle, 0)
+    o_ref[...] = landed_ref[...]
+
+
+def exchange(sent, y, z):
     tables = [jnp.asarray(x) for x in row_tables()]
-    held, section = [previous] if previous is not None else [], chunk % GROUP
     tables[3] = lax.dynamic_index_in_dim(tables[3], z, 0, keepdims=False)
-    t = 4 * y + PER_CHUNK * chunk + jnp.arange(PER_CHUNK, dtype=jnp.int32)
+    t = 4 * y + jnp.arange(CHUNKS, dtype=jnp.int32)
     wave = STEP * (64 * jnp.arange(128, dtype=jnp.int32)[None, :] + t[:, None]).astype(jnp.float32)
-    squares = jnp.broadcast_to((wave * wave)[:, :, None], (PER_CHUNK, 128, 128))
+    squares = jnp.broadcast_to((wave * wave)[:, :, None], (CHUNKS, 128, 128))
+    vmem = pl.BlockSpec(memory_space=pltpu.VMEM)
     return pl.pallas_call(
-        row_kernel,
-        grid=(PER_CHUNK,),
-        in_specs=[
-            pl.BlockSpec((16, None, 2, 128, 128), lambda k: (0, k, 0, 0, 0)),
-            pl.BlockSpec((None, 128, 128), lambda k: (k, 0, 0)),
-        ]
-        + [whole(x.shape) for x in tables]
-        + [pl.BlockSpec(memory_space=pl.ANY)] * len(held),
-        out_specs=pl.BlockSpec((128, ROWS, 128), lambda k: (0, section, 0), pipeline_mode=pl.Buffered(1)),
-        out_shape=jax.ShapeDtypeStruct((128, GROUP * ROWS, 128), jnp.float32),
-        input_output_aliases={7: 0} if held else {},
+        exchange_kernel,
+        in_specs=[pl.BlockSpec(memory_space=pl.ANY)] + [vmem] * (1 + len(tables)),
+        out_specs=vmem,
+        out_shape=jax.ShapeDtypeStruct((COLS, CHUNKS * ROWS, 128), jnp.float32),
         scratch_shapes=[
+            pltpu.VMEM((CHUNKS, COLS, 2, 128, 128), jnp.float32),
+            pltpu.VMEM((CHUNKS, 128, ROWS, 128), jnp.float32),
+            pltpu.VMEM((CHUNKS, LANES, DEEP - 1, 4, ROWS, 128), jnp.float32),
+            pltpu.VMEM((CHUNKS, COLS, ROWS, 128), jnp.float32),
+            pltpu.VMEM((COLS, CHUNKS * ROWS, 128), jnp.float32),
             pltpu.VMEM((8, 16, 16, 768), jnp.bfloat16),
             pltpu.VMEM((256, 256), jnp.float32),
             pltpu.VMEM((256, 256), jnp.float32),
@@ -321,28 +461,25 @@
             pltpu.VMEM((8, 2, 128, 128), jnp.float32),
             pltpu.VMEM((16, 128, 768), jnp.bfloat16),
             pltpu.VMEM((8, 128, 128), jnp.float32),
+            pltpu.SemaphoreType.DMA((CHUNKS,)),
+            pltpu.SemaphoreType.DMA((CHUNKS, COLS)),
+            pltpu.SemaphoreType.DMA((CHUNKS, COLS)),
+            pltpu.SemaphoreType.DMA((CHUNKS, LANES, DEEP - 1)),
+            pltpu.SemaphoreType.DMA((CHUNKS, LANES, DEEP - 1)),
+            pltpu.SemaphoreType.DMA((CHUNKS, COLS)),
+            pltpu.SemaphoreType.DMA((CHUNKS, COLS)),
         ],
-        compiler_params=pltpu.CompilerParams(vmem_limit_bytes=56 << 20),
-        cost_estimate=pl.CostEstimate(flops=PER_CHUNK * 2 * 49152 * 65536, bytes_accessed=16 << 20, transcendentals=0),
-        name="row_stage",
-    )(arrived.reshape(16, PER_CHUNK, 2, 128, 128), squares, *tables, *held)
+        compiler_params=pltpu.CompilerParams(vmem_limit_bytes=63 << 20, collective_id=0, has_side_effects=True),
+        name="exchange",
+    )(sent.reshape(CHUNKS, COLS, 2, 128, 128), squares, *tables)
 
 
 def final_kernel(*refs):
-    count = CHUNKS // GROUP
-    y_refs = [refs[c // GROUP].at[:, pl.ds(c % GROUP * ROWS, ROWS), :] for c in range(CHUNKS)]
-    w_ref, state_ref, k_ref, first_ref, twist_ref, second_ref, scales_ref, o_ref, n_ref, a_ref, r_ref, f_ref = refs[count:]
-    for chunk in range(CHUNKS):
-        for k in range(PER_CHUNK):
-            place = 16 * (chunk * PER_CHUNK + k)
-            for q in range(4):
-                block = y_refs[chunk][:, 32 * k + 8 * q : 32 * k + 8 * q + 8, :]
-                a_ref[8 * q : 8 * q + 8, place : place + 16, :] = jnp.swapaxes(block, 0, 1)
-        block = jnp.swapaxes(y_refs[chunk][:, 32 * PER_CHUNK :, :], 0, 1)
-        for k in range(PER_CHUNK):
-            place = 16 * (chunk * PER_CHUNK + k)
-            for part in range(2):
-                a_ref[32 + part, place : place + 16, :] = block[2 * k + part]
+    y_ref, w_ref, state_ref, k_ref, first_ref, twist_ref, second_ref, scales_ref, o_ref, n_ref, a_ref, r_ref, f_ref = refs
+    for k in range(CHUNKS):
+        for q in range(5):
+            block = jnp.swapaxes(y_ref[:, ROWS * k + 8 * q : ROWS * k + 8 * q + 8, :], 0, 1)
+            a_ref[8 * q : 8 * q + 8, 16 * k : 16 * k + 16, :] = block
 
     def synthesis(pairs):
         high, low = split(jnp.concatenate([jnp.concatenate(p, axis=1) for p in pairs], axis=0))
@@ -411,21 +548,21 @@
     return pl.pallas_call(
         final_kernel,
         grid=(1,),
-        in_specs=[whole((16, GROUP * ROWS, 128))] * (CHUNKS // GROUP)
+        in_specs=[whole((COLS, CHUNKS * ROWS, 128))]
         + [pl.BlockSpec(memory_space=pltpu.SMEM), whole((6, 8, N))]
         + [pl.BlockSpec((8, None, 64, 256), lambda v: (0, 0, 0, 0))]
         + [whole(x.shape) for x in tables],
         out_specs=[whole((5, 8, N)), whole((6, 8, N))],
         out_shape=[jax.ShapeDtypeStruct((5, 8, N), jnp.float32), jax.ShapeDtypeStruct((6, 8, N), jnp.float32)],
         scratch_shapes=[
-            pltpu.VMEM((34, 64, 128), jnp.float32),
+            pltpu.VMEM((40, 64, 128), jnp.float32),
             pltpu.VMEM((64, 256), jnp.float32),
             pltpu.VMEM((5, 8, 64, 256), jnp.float32),
         ],
         compiler_params=pltpu.CompilerParams(vmem_limit_bytes=40 << 20),
         cost_estimate=pl.CostEstimate(flops=2 * 16384 * 65536, bytes_accessed=8 << 20, transcendentals=0),
         name="final_stage",
-    )(*returned, weight, state, rows, *tables)
+    )(returned, weight, state, rows, *tables)
 
 
 def advance_kernel(w_ref, second_ref, s_ref, f_ref, n_ref, o_ref):
@@ -454,25 +591,10 @@
     )(weight, second, received, fields, state)
 
 
-def exchanged(value):
-    return lax.all_to_all(value, "col", split_axis=0, concat_axis=0, tiled=True)
-
-
 def body(convergence, lens_weight, rays_in):
     y, z = lax.axis_index("col"), lax.axis_index("row")
     rows = convergence.reshape(8, 16, 64, 256)
-    sent, summed, returned = [], [], []
-    for chunk in range(CHUNKS):
-        sent.append(forward(rows, chunk))
-    partial = None
-    for chunk in range(CHUNKS):
-        arrived = exchanged(sent[chunk])
-        partial = row_stage(arrived, chunk, y, z, partial)
-        if chunk % GROUP == GROUP - 1:
-            summed.append(lax.psum_scatter(partial, "row", scatter_dimension=0, tiled=True))
-            partial = None
-    for group in range(CHUNKS // GROUP):
-        returned.append(exchanged(summed[group]))
+    returned = exchange(forward(rows), y, z)
     fields, state = final_stage(returned, rows, lens_weight, rays_in)
     received = lax.ppermute(state, "shell", [(0, 1)])
     second = lax.axis_index("shell").astype(jnp.int32).reshape(1)

time: 354 us -> 295 us (0.83)
  waiting for transfers between devices: 115 us -> 20.9 us
  Pallas kernels: 161 us -> 253 us
  starting transfers between devices: 39.6 us -> 1.28 us
  between operations: 14.3 us -> 0.78 us
  local copies, waits for them, and re-layouts: 23.3 us -> 18.9 us
    pallas_call x5 -> x2, Pallas kernels: 116 us -> 231 us  [the longest x1 223 us: exchange(): pl.pallas_call(exchange_kernel, in_specs=[pl.BlockSpec(memory_space=pl.AN...]
    reduce_scatter x2 -> x0, waiting for transfers between devices: 65.6 us -> none  [body(): lax.psum_scatter(partial, 'row', scatter_dimension=0, tiled=True)]
    all_to_all x6 -> x0, waiting for transfers between devices: 41.4 us -> none  [exchanged(): return lax.all_to_all(value, 'col', split_axis=0, concat_axis=0, tiled=True)]
    all_to_all x6 -> x0, starting transfers between devices: 38.2 us -> none  [exchanged(): return lax.all_to_all(value, 'col', split_axis=0, concat_axis=0, tiled=True)]
    pallas_call x4 -> x1, Pallas kernels: 37.3 us -> 14.8 us  [forward(): pl.pallas_call(forward_kernel, grid=(16,), in_specs=[pl.BlockSpec((8, Non...]
    ppermute x1, waiting for transfers between devices: 7.58 us -> 20.9 us  [body(): received = lax.ppermute(state, 'shell', [(0, 1)])]
    unnamed x47 -> x27, local copies, waits for them, and re-layouts: 19 us -> 16.8 us
  transfers between devices with their start and end apart: 9 -> 1, of which waited for: 5 -> 1; matrix products, arithmetic and copies ran while one was open for 1% -> 0% of each run, Pallas kernels for 31% -> 0%
where the time goes in v3:
time: 295 us
  Pallas kernels  253 us (86%)
  waiting for transfers between devices  20.9 us (7%)
  local copies, waits for them, and re-layouts  18.9 us (6%)
    pallas_call x1, Pallas kernels, exchange(): pl.pallas_call(exchange_kernel, in_specs=[pl.BlockSpec(memory_space=pl.AN...  223 us
    ppermute x1, waiting for transfers between devices, body(): received = lax.ppermute(state, 'shell', [(0, 1)])  20.9 us
    unnamed x27, local copies, waits for them, and re-layouts  16.8 us
    pallas_call x1, Pallas kernels, forward(): pl.pallas_call(forward_kernel, grid=(16,), in_specs=[pl.BlockSpec((8, Non...  14.8 us
    pallas_call x1, Pallas kernels, final_stage(): pl.pallas_call(final_kernel, grid=(1,), in_specs=[whole((COLS, CHUNKS * R...  7.72 us
    pallas_call x1, Pallas kernels, advance(): pl.pallas_call(advance_kernel, grid=(N // width,), in_specs=[pl.BlockSpec...  7.35 us
  transfers between devices with their start and end apart: 1, of which 1 were waited for; matrix products, arithmetic and copies ran while one was open for 0% of the time, Pallas kernels for 0%

profile of v3, /device:TPU:1, one launch (start us, length us, event | category | flops | bytes accessed | tf_op | source)
XLA Modules:
  0.0 294.7 jit_solution(5161172179162658126)
XLA Ops:
  0.0 0.0 copy-start.10
  0.0 0.0 copy-start.11
  0.0 0.0 copy-start.12
  0.0 5.5 %copy.16 = bf16[16,8,64,256]{3,2,1,0:T(8,128)(2,1)} copy(bf16[16,8,64,256]{3,1,2,0:T(8,128)(2,1)} %bitcast.12) | data formatting | bytes 8388608
  6.2 1.3 dynamic-slice_bitcast_fusion.back_ref
  7.5 0.1 multiply_multiply_fusion
  7.5 0.0 copy-done.10
  7.5 0.0 copy-done.11
  7.5 0.0 copy-done.12
  7.5 0.0 copy-start
  7.5 2.2 copy-done
  9.7 14.8 %forward.1 = f32[64,2,128,128]{3,2,1,0:T(8,128)S(1)} custom-call(bf16[8,16,64,256]{3,2,1,0:T(8,128)(2,1)S(1)} %bitcast.10, bf16[128,128]{1,0:T(8,128)(2,1)S(1)} %copy-done.12, f32[2,64,256]{2,1,0:T(8,128)S(1)} %copy-done.11, bf16[1536,256]{1,0:T(8,128)(2,1)S(1)} %copy-done.10), custom_call_target="tpu_custom_call" | custom-call | flops 10485760000 | bytes 8388608 | tf_op jit(solution)/shard_map/forward/pallas_call | solution.py:181
  24.6 0.0 copy-start.1
  24.6 3.2 %copy-done.1 = f32[64,2,128,128]{3,2,1,0:T(8,128)} copy-done((f32[64,2,128,128]{3,2,1,0:T(8,128)}, f32[64,2,128,128]{3,2,1,0:T(8,128)S(1)}, u32[]{:S(2)}) %copy-start.1) | copy-done | bytes 8388632
  27.8 0.8 broadcast_in_dim.4.squares_ref
  28.6 0.0 copy-start.7
  28.6 0.0 copy-start.8
  28.6 222.9 %exchange.1.refs_0_ = f32[16,160,128]{2,1,0:T(8,128)} custom-call(f32[4,16,2,128,128]{4,3,2,1,0:T(8,128)} %bitcast.11, f32[4,128,128]{2,1,0:T(8,128)} %broadcast_in_dim.4.squares_ref, bf16[8,768,256]{2,1,0:T(8,128)(2,1)} %constant.53.clone.grid_ref, f32[8,32,128]{2,1,0:T(8,128)} %constant.54.clone.twist_ref, f32[8,40,128]{2,1,0:T(8,128)} %constant.55.clone.waves_ref, ...), custom_call_target="tpu_custom_call" | custom-call | tf_op jit(solution)/shard_map/exchange/pallas_call | solution.py:446
  251.5 0.0 copy-done.7
  251.5 0.0 copy-done.8
  251.5 0.0 copy-done.9
  251.5 0.0 copy-start.2
  251.5 1.3 copy-done.2
  252.9 1.9 copy-done.3
  254.7 1.1 copy-done.6
  255.9 7.7 %final_stage.1 = (f32[5,8,16384]{2,1,0:T(8,128)S(1)}, f32[6,8,16384]{2,1,0:T(8,128)S(1)}) custom-call(f32[16,160,128]{2,1,0:T(8,128)S(1)} %copy-done.2, f32[1]{0:T(128)S(6)} %copy.17.refs_1_.w_ref, f32[6,8,16384]{2,1,0:T(8,128)S(1)} %copy-done.3, bf16[8,16,64,256]{3,2,1,0:T(8,128)(2,1)} %bitcast.9, bf16[768,512]{1,0:T(8,128)(2,1)S(1)} %copy-done.6, ...), custom_call_target="tpu_custom_call" | custom-call | flops 2147483648 | bytes 8388608 | tf_op jit(solution)/shard_map/final_stage/pallas_call | solution.py:548
  263.6 0.0 copy-start.5
  263.6 1.5 copy-done.5
  265.2 1.3 collective-permute-start
  266.4 20.9 %collective-permute-done.s_ref = f32[6,8,16384]{2,1,0:T(8,128)} collective-permute-done((f32[6,8,16384]{2,1,0:T(8,128)S(1)}, f32[6,8,16384]{2,1,0:T(8,128)}, u32[]{:S(2)}, u32[]{:S(2)}) %collective-permute-start) | collective-permute-done | bytes 3145760 | tf_op jit(solution)/shard_map/ppermute | solution.py:599
  287.3 0.0 copy-done.4
  287.3 7.3 %advance.1 = f32[6,8,16384]{2,1,0:T(8,128)} custom-call(f32[1]{0:T(128)S(6)} %copy.17.refs_1_.w_ref, s32[1]{0:T(128)} %bitcast.second_ref, f32[6,8,16384]{2,1,0:T(8,128)} %collective-permute-done.s_ref, f32[5,8,16384]{2,1,0:T(8,128)} %copy-done.5, f32[6,8,16384]{2,1,0:T(8,128)} %copy-done.4), custom_call_target="tpu_custom_call" | custom-call | flops 2883584 | bytes 12058624 | tf_op jit(solution)/shard_map/advance/pallas_call | solution.py:577
  (6 shorter events, 0.0 us)
Async XLA Ops:
  0.0 7.5 %copy-start.10 = (bf16[1536,256]{1,0:T(8,128)(2,1)S(1)}, bf16[1536,256]{1,0:T(8,128)(2,1)}, u32[]{:S(2)}) copy-start(bf16[1536,256]{1,0:T(8,128)(2,1)} %constant.52.clone.second_ref) | copy-start | bytes 2359300
  0.0 7.5 %copy-start.11 = (f32[2,64,256]{2,1,0:T(8,128)S(1)}, f32[2,64,256]{2,1,0:T(8,128)}, u32[]{:S(2)}) copy-start(f32[2,64,256]{2,1,0:T(8,128)} %constant.51.clone.twist_ref) | copy-start | bytes 393220
  0.0 7.5 %copy-start.12 = (bf16[128,128]{1,0:T(8,128)(2,1)S(1)}, bf16[128,128]{1,0:T(8,128)(2,1)}, u32[]{:S(2)}) copy-start(bf16[128,128]{1,0:T(8,128)(2,1)} %constant.50.clone.first_ref) | copy-start | bytes 98308
  7.5 2.2 copy-start
  24.6 3.2 %copy-start.1 = (f32[64,2,128,128]{3,2,1,0:T(8,128)}, f32[64,2,128,128]{3,2,1,0:T(8,128)S(1)}, u32[]{:S(2)}) copy-start(f32[64,2,128,128]{3,2,1,0:T(8,128)S(1)} %forward.1) | copy-start | bytes 25165828
  28.6 222.9 %copy-start.7 = (f32[2,64,256]{2,1,0:T(8,128)S(1)}, f32[2,64,256]{2,1,0:T(8,128)}, u32[]{:S(2)}) copy-start(f32[2,64,256]{2,1,0:T(8,128)} %constant.59.clone.refs_5_) | copy-start | bytes 393220
  28.6 222.9 %copy-start.8 = (f32[3,64,128]{2,1,0:T(8,128)S(1)}, f32[3,64,128]{2,1,0:T(8,128)}, u32[]{:S(2)}) copy-start(f32[3,64,128]{2,1,0:T(8,128)} %constant.61.clone.refs_7_) | copy-start | bytes 294916
  28.6 222.9 %copy-start.9 = (bf16[64,384]{1,0:T(8,128)(2,1)S(1)}, bf16[64,384]{1,0:T(8,128)(2,1)}, u32[]{:S(2)}) copy-start(bf16[64,384]{1,0:T(8,128)(2,1)} %constant.60.clone.refs_6_) | copy-start | bytes 147460
  251.5 1.3 copy-start.2
  252.9 1.9 copy-start.3
  254.7 1.1 copy-start.6
  263.6 1.5 copy-start.5
  265.1 22.2 %copy-start.4 = (f32[6,8,16384]{2,1,0:T(8,128)}, f32[6,8,16384]{2,1,0:T(8,128)S(1)}, u32[]{:S(2)}) copy-start(f32[6,8,16384]{2,1,0:T(8,128)S(1)} %get-tuple-element.7.n_ref) | copy-start | bytes 9437188
  265.2 22.2 %collective-permute-start = (f32[6,8,16384]{2,1,0:T(8,128)S(1)}, f32[6,8,16384]{2,1,0:T(8,128)}, u32[]{:S(2)}, u32[]{:S(2)}) collective-permute-start(f32[6,8,16384]{2,1,0:T(8,128)S(1)} %get-tuple-element.7.n_ref), channel_id=1, source_target_pairs={{0,128},{1,129},{2,130},{3,131},{4,132},{5,133},{6,134},{7,135},{8... | collective-permute-start | bytes 9437192 | tf_op jit(solution)/shard_map/ppermute | solution.py:599

commit v4 on v3

--- a/solution.py
+++ b/solution.py
@@ -374,7 +374,7 @@
         lax.fori_loop(1, COLS, give, 0)
         return 0
 
-    lax.fori_loop(0, CHUNKS, launch, 0)
+    launch(0, 0)
 
     def chunk(k, _):
         own(k).wait()
@@ -384,6 +384,10 @@
             return 0
 
         lax.fori_loop(1, COLS, take, 0)
+
+        @pl.when(k < CHUNKS - 1)
+        def _():
+            launch(k + 1, 0)
 
         @pl.when(k > 0)
         def _():
@@ -475,7 +479,11 @@
 
 
 def final_kernel(*refs):
-    y_ref, w_ref, state_ref, k_ref, first_ref, twist_ref, second_ref, scales_ref, o_ref, n_ref, a_ref, r_ref, f_ref = refs
+    y_ref, w_ref, state_ref, k_ref, first_ref, twist_ref, second_ref, scales_ref, o_ref, a_ref, r_ref, f_ref, held_ref, send_sem, recv_sem = refs
+    shell = lax.axis_index("shell")
+    barrier = pltpu.get_barrier_semaphore()
+    pl.semaphore_signal(barrier, inc=1, device_id={"shell": 1 - shell}, device_id_type=pl.DeviceIdType.MESH)
+    pl.semaphore_wait(barrier, 1)
     for k in range(CHUNKS):
         for q in range(5):
             block = jnp.swapaxes(y_ref[:, ROWS * k + 8 * q : ROWS * k + 8 * q + 8, :], 0, 1)
@@ -516,18 +524,43 @@
 
     lax.fori_loop(0, 8, ray, 0)
 
-    def emit(g, _):
+    def passed(g):
+        part = (slice(None), slice(None), pl.ds(pl.multiple_of(2048 * g, 2048), 2048))
+        return pltpu.make_async_remote_copy(
+            o_ref.at[part], held_ref.at[part], send_sem.at[g], recv_sem.at[g],
+            device_id={"shell": 1 - shell}, device_id_type=pl.DeviceIdType.MESH,
+        )
+
+    def emit(g, source_ref):
         blocks = [jnp.swapaxes(f_ref[f, :, pl.ds(pl.multiple_of(8 * g, 8), 8), :], 0, 1) for f in range(5)]
         for v in range(8):
             place = pl.ds(pl.multiple_of((8 * g + v) * 256, 256), 256)
             fields = [block[v] for block in blocks]
-            for f in range(5):
-                o_ref[f, :, place] = fields[f]
-            for e, value in enumerate(moved([state_ref[e, :, place] for e in range(6)], fields, w_ref[0])):
-                n_ref[e, :, place] = value
-        return 0
-
-    lax.fori_loop(0, 8, emit, 0)
+            for e, value in enumerate(moved([source_ref[e, :, place] for e in range(6)], fields, w_ref[0])):
+                o_ref[e, :, place] = value
+
+    def opening(g, _):
+        emit(g, state_ref)
+        passed(g).start()
+        return 0
+
+    def closing(g, _):
+        passed(g).wait_recv()
+        emit(g, held_ref)
+        return 0
+
+    def settled(g, _):
+        passed(g).wait_send()
+        return 0
+
+    @pl.when(shell == 0)
+    def _():
+        lax.fori_loop(0, 8, opening, 0)
+        lax.fori_loop(0, 8, settled, 0)
+
+    @pl.when(shell == 1)
+    def _():
+        lax.fori_loop(0, 8, closing, 0)
 
 
 def moved(state, fields, w):
@@ -545,60 +578,31 @@
 
 def final_stage(returned, rows, weight, state):
     tables = [jnp.asarray(x) for x in final_tables()]
+    vmem = pl.BlockSpec(memory_space=pltpu.VMEM)
     return pl.pallas_call(
         final_kernel,
-        grid=(1,),
-        in_specs=[whole((COLS, CHUNKS * ROWS, 128))]
-        + [pl.BlockSpec(memory_space=pltpu.SMEM), whole((6, 8, N))]
-        + [pl.BlockSpec((8, None, 64, 256), lambda v: (0, 0, 0, 0))]
-        + [whole(x.shape) for x in tables],
-        out_specs=[whole((5, 8, N)), whole((6, 8, N))],
-        out_shape=[jax.ShapeDtypeStruct((5, 8, N), jnp.float32), jax.ShapeDtypeStruct((6, 8, N), jnp.float32)],
+        in_specs=[vmem, pl.BlockSpec(memory_space=pltpu.SMEM)] + [vmem] * (2 + len(tables)),
+        out_specs=vmem,
+        out_shape=jax.ShapeDtypeStruct((6, 8, N), jnp.float32),
         scratch_shapes=[
             pltpu.VMEM((40, 64, 128), jnp.float32),
             pltpu.VMEM((64, 256), jnp.float32),
             pltpu.VMEM((5, 8, 64, 256), jnp.float32),
+            pltpu.VMEM((6, 8, N), jnp.float32),
+            pltpu.SemaphoreType.DMA((8,)),
+            pltpu.SemaphoreType.DMA((8,)),
         ],
-        compiler_params=pltpu.CompilerParams(vmem_limit_bytes=40 << 20),
-        cost_estimate=pl.CostEstimate(flops=2 * 16384 * 65536, bytes_accessed=8 << 20, transcendentals=0),
+        compiler_params=pltpu.CompilerParams(vmem_limit_bytes=40 << 20, collective_id=1, has_side_effects=True),
         name="final_stage",
     )(returned, weight, state, rows, *tables)
-
-
-def advance_kernel(w_ref, second_ref, s_ref, f_ref, n_ref, o_ref):
-    last = second_ref[0] == 1
-    values = moved([s_ref[e] for e in range(6)], [f_ref[f] for f in range(5)], w_ref[0])
-    for e in range(6):
-        o_ref[e] = jnp.where(last, values[e], n_ref[e])
-
-
-def advance(weight, second, received, fields, state):
-    width = 2048
-    return pl.pallas_call(
-        advance_kernel,
-        grid=(N // width,),
-        in_specs=[
-            pl.BlockSpec(memory_space=pltpu.SMEM),
-            pl.BlockSpec(memory_space=pltpu.SMEM),
-            pl.BlockSpec((6, 8, width), lambda p: (0, 0, p)),
-            pl.BlockSpec((5, 8, width), lambda p: (0, 0, p)),
-            pl.BlockSpec((6, 8, width), lambda p: (0, 0, p)),
-        ],
-        out_specs=pl.BlockSpec((6, 8, width), lambda p: (0, 0, p)),
-        out_shape=jax.ShapeDtypeStruct((6, 8, N), jnp.float32),
-        cost_estimate=pl.CostEstimate(flops=22 * 8 * N, bytes_accessed=23 * 8 * N * 4, transcendentals=0),
-        name="advance",
-    )(weight, second, received, fields, state)
 
 
 def body(convergence, lens_weight, rays_in):
     y, z = lax.axis_index("col"), lax.axis_index("row")
     rows = convergence.reshape(8, 16, 64, 256)
     returned = exchange(forward(rows), y, z)
-    fields, state = final_stage(returned, rows, lens_weight, rays_in)
-    received = lax.ppermute(state, "shell", [(0, 1)])
-    second = lax.axis_index("shell").astype(jnp.int32).reshape(1)
-    return advance(lens_weight, second, received, fields, state)[None]
+    kept = convergence.reshape(8, 16, N)[:, 0].reshape(8, 64, 256)
+    return final_stage(returned, kept, lens_weight, rays_in)[None]
 
 
 def solution(mesh):

time: 295 us -> 284 us (0.963)
  waiting for transfers between devices: 20.9 us -> 0 us
  Pallas kernels: 253 us -> 265 us
    ppermute x1 -> x0, waiting for transfers between devices: 20.9 us -> none  [body(): received = lax.ppermute(state, 'shell', [(0, 1)])]
    pallas_call x2 -> x1, Pallas kernels: 15.1 us -> 26.9 us  [final_stage(): pl.pallas_call(final_kernel, in_specs=[vmem, pl.BlockSpec(memory_space=pl...]
    unnamed x27 -> x23, local copies, waits for them, and re-layouts: 16.8 us -> 12.5 us
  transfers between devices with their start and end apart: 1 -> 0, of which waited for: 1 -> 0; matrix products, arithmetic and copies ran while one was open for 0% -> 0% of each run, Pallas kernels for 0% -> 0%
where the time goes in v4:
time: 284 us; the launch traced here: 283 us
  Pallas kernels  265 us (93%)
  local copies, waits for them, and re-layouts  17.6 us (6%)
    pallas_call x1, Pallas kernels, exchange(): pl.pallas_call(exchange_kernel, in_specs=[pl.BlockSpec(memory_space=pl.AN...  223 us
    pallas_call x1, Pallas kernels, final_stage(): pl.pallas_call(final_kernel, in_specs=[vmem, pl.BlockSpec(memory_space=pl...  26.9 us
    pallas_call x1, Pallas kernels, forward(): pl.pallas_call(forward_kernel, grid=(16,), in_specs=[pl.BlockSpec((8, Non...  14.9 us
    unnamed x23, local copies, waits for them, and re-layouts  12.5 us

profile of v4, /device:TPU:1, one launch (start us, length us, event | category | flops | bytes accessed | tf_op | source)
XLA Modules:
  0.0 283.5 jit_solution(15315395879281963212)
XLA Ops:
  0.0 0.0 copy-start.7
  0.0 0.0 copy-start.8
  0.0 0.0 copy-start.9
  0.0 3.5 %copy.18 = bf16[16,8,64,256]{3,2,1,0:T(8,128)(2,1)S(1)} copy(bf16[16,8,64,256]{3,1,2,0:T(8,128)(2,1)} %bitcast.17) | data formatting | bytes 8388608
  3.5 0.0 copy-done.7
  3.5 0.0 copy-done.8
  3.5 0.0 copy-done.9
  3.5 14.9 %forward.1 = f32[64,2,128,128]{3,2,1,0:T(8,128)S(1)} custom-call(bf16[8,16,64,256]{3,2,1,0:T(8,128)(2,1)S(1)} %bitcast.15, bf16[128,128]{1,0:T(8,128)(2,1)S(1)} %copy-done.9, f32[2,64,256]{2,1,0:T(8,128)S(1)} %copy-done.8, bf16[1536,256]{1,0:T(8,128)(2,1)S(1)} %copy-done.7), custom_call_target="tpu_custom_call" | custom-call | flops 10485760000 | bytes 8388608 | tf_op jit(solution)/shard_map/forward/pallas_call | solution.py:181
  18.4 0.0 copy-start
  18.4 3.2 %copy-done = f32[64,2,128,128]{3,2,1,0:T(8,128)} copy-done((f32[64,2,128,128]{3,2,1,0:T(8,128)}, f32[64,2,128,128]{3,2,1,0:T(8,128)S(1)}, u32[]{:S(2)}) %copy-start) | copy-done | bytes 8388632
  21.6 0.1 multiply_multiply_fusion
  21.7 0.8 broadcast_in_dim.4.squares_ref
  22.6 1.3 dynamic-slice_bitcast_fusion.back_ref
  23.9 0.0 copy-start.3
  23.9 0.0 copy-start.4
  23.9 0.0 copy-start.6
  23.9 223.3 %exchange.1.refs_0_ = f32[16,160,128]{2,1,0:T(8,128)} custom-call(f32[4,16,2,128,128]{4,3,2,1,0:T(8,128)} %bitcast.14, f32[4,128,128]{2,1,0:T(8,128)} %broadcast_in_dim.4.squares_ref, bf16[8,768,256]{2,1,0:T(8,128)(2,1)} %constant.48.clone.grid_ref, f32[8,32,128]{2,1,0:T(8,128)} %constant.49.clone.twist_ref, f32[8,40,128]{2,1,0:T(8,128)} %constant.50.clone.waves_ref, ...), custom_call_target="tpu_custom_call" | custom-call | tf_op jit(solution)/shard_map/exchange/pallas_call | solution.py:450
  247.8 2.9 %slice_reduce_fusion = bf16[8,16384]{1,0:T(8,128)(2,1)S(1)} fusion(bf16[8,16,16384]{2,1,0:T(8,128)(2,1)} %bitcast.18), kind=kLoop, calls=%fused_computation | loop fusion | bytes 524288 | tf_op jit(solution)/shard_map/slice | solution.py:604
  250.8 0.0 copy-done.3
  250.8 0.0 copy-done.4
  250.8 0.0 copy-done.6
  250.8 0.0 copy-start.1
  250.8 1.3 copy-done.1
  252.2 0.0 copy-start.2
  252.2 1.9 copy-done.2
  254.0 0.0 copy-start.5
  254.0 0.9 copy-done.5
  254.9 26.9 %final_stage.1 = f32[6,8,16384]{2,1,0:T(8,128)S(1)} custom-call(f32[16,160,128]{2,1,0:T(8,128)S(1)} %copy-done.1, f32[1]{0:T(128)S(6)} %copy.23.refs_1_, f32[6,8,16384]{2,1,0:T(8,128)S(1)} %copy-done.2, bf16[8,64,256]{2,1,0:T(8,128)(2,1)S(1)} %bitcast.16, bf16[768,512]{1,0:T(8,128)(2,1)S(1)} %copy-done.3, f32[2,64,256]{2,1,0:T(8,128)S(1)} %copy-done.4, ...), custom_call_target="tpu_custom_call" | custom-call | tf_op jit(solution)/shard_map/final_stage/pallas_call | solution.py:582
  281.8 1.7 copy.24
  (3 shorter events, 0.1 us)
Async XLA Ops:
  0.0 3.5 %copy-start.7 = (bf16[1536,256]{1,0:T(8,128)(2,1)S(1)}, bf16[1536,256]{1,0:T(8,128)(2,1)}, u32[]{:S(2)}) copy-start(bf16[1536,256]{1,0:T(8,128)(2,1)} %constant.47.clone.second_ref) | copy-start | bytes 2359300
  0.0 3.5 %copy-start.8 = (f32[2,64,256]{2,1,0:T(8,128)S(1)}, f32[2,64,256]{2,1,0:T(8,128)}, u32[]{:S(2)}) copy-start(f32[2,64,256]{2,1,0:T(8,128)} %constant.46.clone.twist_ref) | copy-start | bytes 393220
  0.0 3.5 %copy-start.9 = (bf16[128,128]{1,0:T(8,128)(2,1)S(1)}, bf16[128,128]{1,0:T(8,128)(2,1)}, u32[]{:S(2)}) copy-start(bf16[128,128]{1,0:T(8,128)(2,1)} %constant.45.clone.first_ref) | copy-start | bytes 98308
  18.4 3.2 %copy-start = (f32[64,2,128,128]{3,2,1,0:T(8,128)}, f32[64,2,128,128]{3,2,1,0:T(8,128)S(1)}, u32[]{:S(2)}) copy-start(f32[64,2,128,128]{3,2,1,0:T(8,128)S(1)} %forward.1) | copy-start | bytes 25165828
  23.9 226.9 %copy-start.3 = (bf16[768,512]{1,0:T(8,128)(2,1)S(1)}, bf16[768,512]{1,0:T(8,128)(2,1)}, u32[]{:S(2)}) copy-start(bf16[768,512]{1,0:T(8,128)(2,1)} %constant.53.clone.refs_4_) | copy-start | bytes 2359300
  23.9 227.0 %copy-start.4 = (f32[2,64,256]{2,1,0:T(8,128)S(1)}, f32[2,64,256]{2,1,0:T(8,128)}, u32[]{:S(2)}) copy-start(f32[2,64,256]{2,1,0:T(8,128)} %constant.54.clone.refs_5_) | copy-start | bytes 393220
  23.9 227.0 %copy-start.6 = (bf16[64,384]{1,0:T(8,128)(2,1)S(1)}, bf16[64,384]{1,0:T(8,128)(2,1)}, u32[]{:S(2)}) copy-start(bf16[64,384]{1,0:T(8,128)(2,1)} %constant.55.clone.refs_6_) | copy-start | bytes 147460
  250.8 1.3 copy-start.1
  252.2 1.9 copy-start.2
  254.0 0.9 copy-start.5

commit v5 on v4

--- a/solution.py
+++ b/solution.py
@@ -16,7 +16,7 @@
 ROWS = 40
 COLS = 16
 DEEP = 8
-LANES = 4
+LANES = 8
 STEP = 2.0 * math.pi / N
 
 
@@ -190,7 +190,7 @@
         out_specs=pl.BlockSpec((HELD, 2, 8, 128), lambda v: (0, 0, v, 0)),
         out_shape=jax.ShapeDtypeStruct((HELD, 2, 128, 128), jnp.float32),
         scratch_shapes=[pltpu.VMEM((8 * HELD, 1536), jnp.bfloat16)],
-        compiler_params=pltpu.CompilerParams(vmem_limit_bytes=40 << 20),
+        compiler_params=pltpu.CompilerParams(vmem_limit_bytes=62 << 20),
         cost_estimate=pl.CostEstimate(flops=2 * 128 * HELD * 2500 * 256, bytes_accessed=8 << 20, transcendentals=0),
         name="forward",
     )(rows, first, twist, second)
@@ -327,7 +327,7 @@
         )
 
     def share(block, lane):
-        return pl.ds(lax.rem(block + 2 * DEEP, DEEP) * COLS + 4 * lane, 4)
+        return pl.ds(lax.rem(block + 2 * DEEP, DEEP) * COLS + 2 * lane, 2)
 
     def ring(k, lane, s, source):
         return pltpu.make_async_remote_copy(
@@ -353,7 +353,7 @@
 
             @pl.when(s == DEEP - 2)
             def _():
-                reduced_ref[k, 4 * lane : 4 * lane + 4] = total
+                reduced_ref[k, 2 * lane : 2 * lane + 2] = total
 
     def close_ring(k):
         landed_ref[y, pl.ds(pl.multiple_of(k * ROWS, 8), ROWS), :] = reduced_ref[k, y]
@@ -385,38 +385,53 @@
 
         lax.fori_loop(1, COLS, take, 0)
 
-        @pl.when(k < CHUNKS - 1)
+        @pl.when(k == 0)
         def _():
-            launch(k + 1, 0)
+            launch(1, 0)
 
         @pl.when(k > 0)
         def _():
             open_ring(k - 1)
 
-        def between(s):
-            @pl.when(k > 0)
+        def between(g):
+            @pl.when((k > 0) & (g % 2 == 0))
             def _():
-                step(k - 1, s)
+                step(k - 1, g // 2)
+
+            @pl.when((k > 1) & (g % 2 == 1))
+            def _():
+                step(k - 2, 4 + g // 2)
+
+            @pl.when((k < CHUNKS - 2) & (g == 5))
+            def _():
+                launch(k + 2, 0)
 
         row_chunk(
             arrived_ref.at[k], squares_ref.at[k], grid_ref, twist_ref, waves_ref, back_ref, left_ref,
             partial_ref.at[k], l_ref, z0_ref, z1_ref, s_ref, q_ref, g_ref, r_ref, between,
         )
 
-        @pl.when(k > 0)
+        @pl.when(k > 1)
         def _():
-            close_ring(k - 1)
+            close_ring(k - 2)
 
         return 0
 
     lax.fori_loop(0, CHUNKS, chunk, 0)
     open_ring(CHUNKS - 1)
 
+    def both(s, _):
+        step(CHUNKS - 2, 4 + s)
+        step(CHUNKS - 1, s)
+        return 0
+
     def last(s, _):
         step(CHUNKS - 1, s)
         return 0
 
-    lax.fori_loop(0, DEEP - 1, last, 0)
+    lax.fori_loop(0, 3, both, 0)
+    close_ring(CHUNKS - 2)
+    lax.fori_loop(3, DEEP - 1, last, 0)
     close_ring(CHUNKS - 1)
 
     def settle(k, _):
@@ -455,7 +470,7 @@
         scratch_shapes=[
             pltpu.VMEM((CHUNKS, COLS, 2, 128, 128), jnp.float32),
             pltpu.VMEM((CHUNKS, 128, ROWS, 128), jnp.float32),
-            pltpu.VMEM((CHUNKS, LANES, DEEP - 1, 4, ROWS, 128), jnp.float32),
+            pltpu.VMEM((CHUNKS, LANES, DEEP - 1, 2, ROWS, 128), jnp.float32),
             pltpu.VMEM((CHUNKS, COLS, ROWS, 128), jnp.float32),
             pltpu.VMEM((COLS, CHUNKS * ROWS, 128), jnp.float32),
             pltpu.VMEM((8, 16, 16, 768), jnp.bfloat16),
@@ -479,11 +494,19 @@
 
 
 def final_kernel(*refs):
-    y_ref, w_ref, state_ref, k_ref, first_ref, twist_ref, second_ref, scales_ref, o_ref, a_ref, r_ref, f_ref, held_ref, send_sem, recv_sem = refs
+    y_ref, w_ref, state_hbm, rows_hbm, first_ref, twist_ref, second_ref, scales_ref, o_ref, a_ref, r_ref, f_ref, held_ref, send_sem, recv_sem, load_sem, k_ref, kept_sem = refs
+    kept = pltpu.make_async_copy(rows_hbm.at[:, 0], k_ref, kept_sem)
+    kept.start()
     shell = lax.axis_index("shell")
     barrier = pltpu.get_barrier_semaphore()
     pl.semaphore_signal(barrier, inc=1, device_id={"shell": 1 - shell}, device_id_type=pl.DeviceIdType.MESH)
     pl.semaphore_wait(barrier, 1)
+    loaded = pltpu.make_async_copy(state_hbm, held_ref, load_sem)
+
+    @pl.when(shell == 0)
+    def _():
+        loaded.start()
+
     for k in range(CHUNKS):
         for q in range(5):
             block = jnp.swapaxes(y_ref[:, ROWS * k + 8 * q : ROWS * k + 8 * q + 8, :], 0, 1)
@@ -522,6 +545,7 @@
             f_ref[f, i] = field
         return 0
 
+    kept.wait()
     lax.fori_loop(0, 8, ray, 0)
 
     def passed(g):
@@ -540,7 +564,7 @@
                 o_ref[e, :, place] = value
 
     def opening(g, _):
-        emit(g, state_ref)
+        emit(g, held_ref)
         passed(g).start()
         return 0
 
@@ -555,6 +579,7 @@
 
     @pl.when(shell == 0)
     def _():
+        loaded.wait()
         lax.fori_loop(0, 8, opening, 0)
         lax.fori_loop(0, 8, settled, 0)
 
@@ -581,7 +606,8 @@
     vmem = pl.BlockSpec(memory_space=pltpu.VMEM)
     return pl.pallas_call(
         final_kernel,
-        in_specs=[vmem, pl.BlockSpec(memory_space=pltpu.SMEM)] + [vmem] * (2 + len(tables)),
+        in_specs=[vmem, pl.BlockSpec(memory_space=pltpu.SMEM), pl.BlockSpec(memory_space=pl.ANY), pl.BlockSpec(memory_space=pl.ANY)]
+        + [vmem] * len(tables),
         out_specs=vmem,
         out_shape=jax.ShapeDtypeStruct((6, 8, N), jnp.float32),
         scratch_shapes=[
@@ -591,6 +617,9 @@
             pltpu.VMEM((6, 8, N), jnp.float32),
             pltpu.SemaphoreType.DMA((8,)),
             pltpu.SemaphoreType.DMA((8,)),
+            pltpu.SemaphoreType.DMA,
+            pltpu.VMEM((8, 64, 256), jnp.bfloat16),
+            pltpu.SemaphoreType.DMA,
         ],
         compiler_params=pltpu.CompilerParams(vmem_limit_bytes=40 << 20, collective_id=1, has_side_effects=True),
         name="final_stage",
@@ -601,8 +630,7 @@
     y, z = lax.axis_index("col"), lax.axis_index("row")
     rows = convergence.reshape(8, 16, 64, 256)
     returned = exchange(forward(rows), y, z)
-    kept = convergence.reshape(8, 16, N)[:, 0].reshape(8, 64, 256)
-    return final_stage(returned, kept, lens_weight, rays_in)[None]
+    return final_stage(returned, rows, lens_weight, rays_in)[None]
 
 
 def solution(mesh):

time: 284 us -> 271 us (0.954)
  Pallas kernels: 265 us -> 254 us
    pallas_call x1, Pallas kernels: 223 us -> 210 us  [exchange(): pl.pallas_call(exchange_kernel, in_specs=[pl.BlockSpec(memory_space=pl.AN...]
    pallas_call x1, Pallas kernels: 14.9 us -> 17.9 us  [forward(): pl.pallas_call(forward_kernel, grid=(16,), in_specs=[pl.BlockSpec((8, Non...]
    slice x1 -> x0, local copies, waits for them, and re-layouts: 2.9 us -> none  [body(): kept = convergence.reshape(8, 16, N)[:, 0].reshape(8, 64, 256)]
    unnamed x23 -> x16, local copies, waits for them, and re-layouts: 12.5 us -> 13.3 us
where the time goes in v5:
time: 271 us; the launch traced here: 270 us
  Pallas kernels  254 us (94%)
  local copies, waits for them, and re-layouts  15.5 us (6%)
    pallas_call x1, Pallas kernels, exchange(): pl.pallas_call(exchange_kernel, in_specs=[pl.BlockSpec(memory_space=pl.AN...  210 us
    pallas_call x1, Pallas kernels, final_stage(): pl.pallas_call(final_kernel, in_specs=[vmem, pl.BlockSpec(memory_space=pl...  25.6 us
    pallas_call x1, Pallas kernels, forward(): pl.pallas_call(forward_kernel, grid=(16,), in_specs=[pl.BlockSpec((8, Non...  17.9 us
    unnamed x16, local copies, waits for them, and re-layouts  13.3 us

profile of v5, /device:TPU:1, one launch (start us, length us, event | category | flops | bytes accessed | tf_op | source)
XLA Modules:
  0.0 270.1 jit_solution(306934160477388496)
XLA Ops:
  0.0 1.3 dynamic-slice_bitcast_fusion.back_ref
  1.3 5.4 %copy.16 = bf16[16,8,64,256]{3,2,1,0:T(8,128)(2,1)} copy(bf16[16,8,64,256]{3,1,2,0:T(8,128)(2,1)} %bitcast.12) | data formatting | bytes 8388608
  6.7 17.9 %forward.1 = f32[64,2,128,128]{3,2,1,0:T(8,128)} custom-call(bf16[8,16,64,256]{3,2,1,0:T(8,128)(2,1)} %bitcast.8, bf16[128,128]{1,0:T(8,128)(2,1)} %constant.45.clone.first_ref, f32[2,64,256]{2,1,0:T(8,128)} %constant.46.clone.twist_ref, bf16[1536,256]{1,0:T(8,128)(2,1)} %constant.47.clone.second_ref), custom_call_target="tpu_custom_call" | custom-call | flops 10485760000 | bytes 8388608 | tf_op jit(solution)/shard_map/forward/pallas_call | solution.py:181
  24.6 0.1 multiply_multiply_fusion
  24.7 0.8 broadcast_in_dim.4.squares_ref
  25.5 0.0 copy-start.3
  25.5 0.0 copy-start.4
  25.6 0.0 copy-start.6
  25.6 210.2 %exchange.1.refs_0_ = f32[16,160,128]{2,1,0:T(8,128)} custom-call(f32[4,16,2,128,128]{4,3,2,1,0:T(8,128)} %bitcast.11, f32[4,128,128]{2,1,0:T(8,128)} %broadcast_in_dim.4.squares_ref, bf16[8,768,256]{2,1,0:T(8,128)(2,1)} %constant.48.clone.grid_ref, f32[8,32,128]{2,1,0:T(8,128)} %constant.49.clone.twist_ref, f32[8,40,128]{2,1,0:T(8,128)} %constant.50.clone.waves_ref, ...), custom_call_target="tpu_custom_call" | custom-call | tf_op jit(solution)/shard_map/exchange/pallas_call | solution.py:465
  236.4 0.0 copy-done.3
  236.4 0.0 copy-done.4
  236.4 0.0 copy-done.6
  236.5 0.0 copy-start
  236.5 2.2 copy-done
  238.6 0.0 copy-start.1
  238.6 1.3 copy-done.1
  240.0 0.0 copy-start.2
  240.0 1.9 copy-done.2
  241.8 0.0 copy-start.5
  241.8 0.9 copy-done.5
  242.7 25.6 %final_stage.1 = f32[6,8,16384]{2,1,0:T(8,128)S(1)} custom-call(f32[16,160,128]{2,1,0:T(8,128)S(1)} %copy-done.1, f32[1]{0:T(128)S(6)} %copy.18.refs_1_, f32[6,8,16384]{2,1,0:T(8,128)S(1)} %copy-done.2, bf16[8,16,64,256]{3,2,1,0:T(8,128)(2,1)S(1)} %bitcast.9, bf16[768,512]{1,0:T(8,128)(2,1)S(1)} %copy-done.3, f32[2,64,256]{2,1,0:T(8,128)S(1)} %copy-done.4, ...), custom_call_target="tpu_custom_call" | custom-call | tf_op jit(solution)/shard_map/final_stage/pallas_call | solution.py:607
  268.4 1.7 copy.19
  (2 shorter events, 0.0 us)
Async XLA Ops:
  25.5 210.9 %copy-start.3 = (bf16[768,512]{1,0:T(8,128)(2,1)S(1)}, bf16[768,512]{1,0:T(8,128)(2,1)}, u32[]{:S(2)}) copy-start(bf16[768,512]{1,0:T(8,128)(2,1)} %constant.53.clone.refs_4_) | copy-start | bytes 2359300
  25.5 210.9 %copy-start.4 = (f32[2,64,256]{2,1,0:T(8,128)S(1)}, f32[2,64,256]{2,1,0:T(8,128)}, u32[]{:S(2)}) copy-start(f32[2,64,256]{2,1,0:T(8,128)} %constant.54.clone.refs_5_) | copy-start | bytes 393220
  25.6 210.9 %copy-start.6 = (bf16[64,384]{1,0:T(8,128)(2,1)S(1)}, bf16[64,384]{1,0:T(8,128)(2,1)}, u32[]{:S(2)}) copy-start(bf16[64,384]{1,0:T(8,128)(2,1)} %constant.55.clone.refs_6_) | copy-start | bytes 147460
  236.5 2.2 copy-start
  238.6 1.3 copy-start.1
  240.0 1.9 copy-start.2
  241.8 0.9 copy-start.5

commit v6 on v5

--- a/solution.py
+++ b/solution.py
@@ -227,7 +227,7 @@
             s_ref[f, j, rows, :] = totals[f]
 
 
-def row_chunk(x_ref, squares_ref, grid_ref, twist_ref, waves_ref, back_ref, left_ref, o_ref, l_ref, z0_ref, z1_ref, s_ref, q_ref, g_ref, r_ref, between):
+def row_chunk(x_ref, squares_ref, grid_ref, twist_ref, waves_ref, back_ref, left_ref, o_ref, l_ref, z0_ref, z1_ref, s_ref, q_ref, g_ref, r_ref, line_ref, between):
     def arrange(v, _):
         rows = pl.ds(pl.multiple_of(v * 8, 8), 8)
         real = x_ref[:, 0, rows, :].reshape(128, 128)
@@ -287,13 +287,13 @@
         line = q_ref[0, part].T[0:1] * (1.0 / N / N)
         place = lax.broadcasted_iota(jnp.int32, (8, 128), 0) == part
         lines = lines + jnp.where(place, jnp.broadcast_to(line, (8, 128)), 0.0)
-    o_ref[:, 32:40, :] = jnp.broadcast_to(lines[None], (128, 8, 128))
+    line_ref[...] = lines
 
 
 def exchange_kernel(
     sent_ref, squares_ref, grid_ref, twist_ref, waves_ref, back_ref, left_ref, o_ref,
-    arrived_ref, partial_ref, slot_ref, reduced_ref, landed_ref, l_ref, z0_ref, z1_ref, s_ref, q_ref, g_ref, r_ref,
-    own_sem, in_send, in_recv, ring_send, ring_recv, back_send, back_recv,
+    arrived_ref, partial_ref, lines_ref, slot_ref, turn_ref, reduced_ref, landed_ref, l_ref, z0_ref, z1_ref, s_ref, q_ref, g_ref, r_ref,
+    own_sem, in_send, in_recv, ring_send, ring_recv, turn_send, turn_recv, back_send, back_recv,
 ):
     y, z = lax.axis_index("col"), lax.axis_index("row")
     right, left = lax.rem(z + 1, DEEP), lax.rem(z + DEEP - 1, DEEP)
@@ -335,12 +335,31 @@
             device_id={"row": right if lane % 2 == 0 else left}, device_id_type=pl.DeviceIdType.MESH,
         )
 
+    def turn(k, s, source):
+        return pltpu.make_async_remote_copy(
+            source, turn_ref.at[k, s], turn_send.at[k, s], turn_recv.at[k, s],
+            device_id={"row": right}, device_id_type=pl.DeviceIdType.MESH,
+        )
+
     def open_ring(k):
+        turn(k, 0, lines_ref.at[k]).start()
         for lane in range(LANES):
             block = z - 1 if lane % 2 == 0 else z + 1
             ring(k, lane, 0, partial_ref.at[k, share(block, lane)]).start()
 
     def step(k, s):
+        turn(k, s, turn_ref.at[k, s]).wait_recv()
+        lines = turn_ref[k, s] + lines_ref[k]
+
+        @pl.when(s < DEEP - 2)
+        def _():
+            turn_ref[k, s] = lines
+            turn(k, s + 1, turn_ref.at[k, s]).start()
+
+        @pl.when(s == DEEP - 2)
+        def _():
+            reduced_ref[k, :, 32:40] = jnp.broadcast_to(lines[None], (COLS, 8, 128))
+
         for lane in range(LANES):
             ring(k, lane, s, slot_ref.at[k, lane, s]).wait_recv()
             block = z - s - 2 if lane % 2 == 0 else z + s + 2
@@ -353,7 +372,7 @@
 
             @pl.when(s == DEEP - 2)
             def _():
-                reduced_ref[k, 2 * lane : 2 * lane + 2] = total
+                reduced_ref[k, 2 * lane : 2 * lane + 2, 0:32] = total
 
     def close_ring(k):
         landed_ref[y, pl.ds(pl.multiple_of(k * ROWS, 8), ROWS), :] = reduced_ref[k, y]
@@ -408,7 +427,7 @@
 
         row_chunk(
             arrived_ref.at[k], squares_ref.at[k], grid_ref, twist_ref, waves_ref, back_ref, left_ref,
-            partial_ref.at[k], l_ref, z0_ref, z1_ref, s_ref, q_ref, g_ref, r_ref, between,
+            partial_ref.at[k], l_ref, z0_ref, z1_ref, s_ref, q_ref, g_ref, r_ref, lines_ref.at[k], between,
         )
 
         @pl.when(k > 1)
@@ -444,6 +463,7 @@
         lax.fori_loop(1, COLS, one, 0)
 
         def two(s, _):
+            turn(k, s, turn_ref.at[k, s]).wait_send()
             for lane in range(LANES):
                 ring(k, lane, s, slot_ref.at[k, lane, s]).wait_send()
             return 0
@@ -469,8 +489,10 @@
         out_shape=jax.ShapeDtypeStruct((COLS, CHUNKS * ROWS, 128), jnp.float32),
         scratch_shapes=[
             pltpu.VMEM((CHUNKS, COLS, 2, 128, 128), jnp.float32),
-            pltpu.VMEM((CHUNKS, 128, ROWS, 128), jnp.float32),
-            pltpu.VMEM((CHUNKS, LANES, DEEP - 1, 2, ROWS, 128), jnp.float32),
+            pltpu.VMEM((CHUNKS, 128, 32, 128), jnp.float32),
+            pltpu.VMEM((CHUNKS, 8, 128), jnp.float32),
+            pltpu.VMEM((CHUNKS, LANES, DEEP - 1, 2, 32, 128), jnp.float32),
+            pltpu.VMEM((CHUNKS, DEEP - 1, 8, 128), jnp.float32),
             pltpu.VMEM((CHUNKS, COLS, ROWS, 128), jnp.float32),
             pltpu.VMEM((COLS, CHUNKS * ROWS, 128), jnp.float32),
             pltpu.VMEM((8, 16, 16, 768), jnp.bfloat16),
@@ -485,6 +507,8 @@
             pltpu.SemaphoreType.DMA((CHUNKS, COLS)),
             pltpu.SemaphoreType.DMA((CHUNKS, LANES, DEEP - 1)),
             pltpu.SemaphoreType.DMA((CHUNKS, LANES, DEEP - 1)),
+            pltpu.SemaphoreType.DMA((CHUNKS, DEEP - 1)),
+            pltpu.SemaphoreType.DMA((CHUNKS, DEEP - 1)),
             pltpu.SemaphoreType.DMA((CHUNKS, COLS)),
             pltpu.SemaphoreType.DMA((CHUNKS, COLS)),
         ],
@@ -621,7 +645,7 @@
             pltpu.VMEM((8, 64, 256), jnp.bfloat16),
             pltpu.SemaphoreType.DMA,
         ],
-        compiler_params=pltpu.CompilerParams(vmem_limit_bytes=40 << 20, collective_id=1, has_side_effects=True),
+        compiler_params=pltpu.CompilerParams(vmem_limit_bytes=62 << 20, collective_id=1, has_side_effects=True),
         name="final_stage",
     )(returned, weight, state, rows, *tables)
 

time: 271 us -> 260 us (0.959)
  Pallas kernels: 254 us -> 247 us
  local copies, waits for them, and re-layouts: 15.5 us -> 11.3 us
    pallas_call x1, Pallas kernels: 210 us -> 203 us  [exchange(): pl.pallas_call(exchange_kernel, in_specs=[pl.BlockSpec(memory_space=pl.AN...]
    unnamed x16 -> x2, local copies, waits for them, and re-layouts: 13.3 us -> 9.15 us
where the time goes in v6:
time: 260 us; the launch traced here: 259 us
  Pallas kernels  247 us (95%)
  local copies, waits for them, and re-layouts  11.3 us (4%)
    pallas_call x1, Pallas kernels, exchange(): pl.pallas_call(exchange_kernel, in_specs=[pl.BlockSpec(memory_space=pl.AN...  203 us
    pallas_call x1, Pallas kernels, final_stage(): pl.pallas_call(final_kernel, in_specs=[vmem, pl.BlockSpec(memory_space=pl...  26.6 us
    pallas_call x1, Pallas kernels, forward(): pl.pallas_call(forward_kernel, grid=(16,), in_specs=[pl.BlockSpec((8, Non...  17.9 us
    unnamed x2, local copies, waits for them, and re-layouts  9.15 us

profile of v6, /device:TPU:1, one launch (start us, length us, event | category | flops | bytes accessed | tf_op | source)
XLA Modules:
  0.0 259.2 jit_solution(17793924794548410417)
XLA Ops:
  0.0 1.3 dynamic-slice_bitcast_fusion.back_ref
  1.3 5.4 %copy.16 = bf16[16,8,64,256]{3,2,1,0:T(8,128)(2,1)} copy(bf16[16,8,64,256]{3,1,2,0:T(8,128)(2,1)} %bitcast.12) | data formatting | bytes 8388608
  6.7 17.9 %forward.1 = f32[64,2,128,128]{3,2,1,0:T(8,128)} custom-call(bf16[8,16,64,256]{3,2,1,0:T(8,128)(2,1)} %bitcast.8, bf16[128,128]{1,0:T(8,128)(2,1)} %constant.45.clone.first_ref, f32[2,64,256]{2,1,0:T(8,128)} %constant.46.clone.twist_ref, bf16[1536,256]{1,0:T(8,128)(2,1)} %constant.47.clone.second_ref), custom_call_target="tpu_custom_call" | custom-call | flops 10485760000 | bytes 8388608 | tf_op jit(solution)/shard_map/forward/pallas_call | solution.py:181
  24.6 0.1 multiply_multiply_fusion
  24.7 0.8 broadcast_in_dim.4.squares_ref
  25.5 202.7 %exchange.1.refs_0_ = f32[16,160,128]{2,1,0:T(8,128)} custom-call(f32[4,16,2,128,128]{4,3,2,1,0:T(8,128)} %bitcast.11, f32[4,128,128]{2,1,0:T(8,128)} %broadcast_in_dim.4.squares_ref, bf16[8,768,256]{2,1,0:T(8,128)(2,1)} %constant.48.clone.grid_ref, f32[8,32,128]{2,1,0:T(8,128)} %constant.49.clone.twist_ref, f32[8,40,128]{2,1,0:T(8,128)} %constant.50.clone.waves_ref, ...), custom_call_target="tpu_custom_call" | custom-call | tf_op jit(solution)/shard_map/exchange/pallas_call | solution.py:485
  228.9 26.6 %final_stage.1 = f32[6,8,16384]{2,1,0:T(8,128)} custom-call(f32[16,160,128]{2,1,0:T(8,128)} %exchange.1.refs_0_, f32[1]{0:T(128)S(6)} %copy.18.refs_1_, f32[6,8,16384]{2,1,0:T(8,128)} %refs_2_.1, bf16[8,16,64,256]{3,2,1,0:T(8,128)(2,1)} %bitcast.9, bf16[768,512]{1,0:T(8,128)(2,1)} %constant.53.clone.refs_4_, f32[2,64,256]{2,1,0:T(8,128)} %constant.54.clone.refs_5_, ...), custom_call_target="tpu_custom_call" | custom-call | tf_op jit(solution)/shard_map/final_stage/pallas_call | solution.py:631
  255.5 3.8 %copy.19 = f32[1,6,8,16384]{3,2,1,0:T(8,128)} copy(f32[1,6,8,16384]{3,2,1,0:T(8,128)} %bitcast.10) | data formatting | bytes 6291456
  (2 shorter events, 0.0 us)
